TPU v7x, 32 devices: a whole 2x2x4 slice. The times are simulated.
32 devices in a mesh: groups: 2 (over x), expert: 16 (over z, y, core).
Axes of the slice: x: 2, y: 2, z: 4, core: 2. Of those that a mesh axis runs over, the one named last changes fastest.
Arguments:
- tokens: bfloat16 [2, 2048, 2048], P(None, ('groups', 'expert')), parts along dimension 1, may hold values from -6 to 6
- w_gate: bfloat16 [16, 2048, 768], P('expert'), may hold values from -0.125 to 0.125
- w_up: bfloat16 [16, 2048, 768], P('expert'), may hold values from -0.125 to 0.125
- w_down: bfloat16 [16, 768, 2048], P('expert'), may hold values from -0.21875 to 0.21875
- hot_gate: bfloat16 [2, 2048, 768], P(None, None, 'expert'), may hold values from -0.125 to 0.125
- hot_up: bfloat16 [2, 2048, 768], P(None, None, 'expert'), may hold values from -0.125 to 0.125
- hot_down: bfloat16 [2, 2048, 768], P(None, None, 'expert'), may hold values from -0.21875 to 0.21875
- cold_routes: int32 [2, 2048, 7], P(None, ('groups', 'expert')), parts along dimension 1, may hold values from 0 to 15, all different within a row; in each aligned block of 64 rows (0 to 63, 64 to 127, ..., all dimensions but the last counted through in order) at most 43 rows name the same one
- hot_pick: int32 [2, 2048], P(None, ('groups', 'expert')), parts along dimension 1, may hold values from 0 to 1, as said below
- gates: float32 [2, 2048, 8], P(None, ('groups', 'expert')), parts along dimension 1, may hold values from 0.1 to 1
Outputs:
- mixed: bfloat16 [2, 2048, 2048], P(None, ('groups', 'expert')), parts along dimension 1
There are 2 independent parts, one for each index of `groups`. A program takes and returns all parts, laid end to end along the dimension named above; an argument that names none is the same for every part. Nothing has to cross between parts.
Inputs may be any that keep to these rules, and one draw needn't show every extreme that they name: `hot_pick`: in each aligned block of 64 tokens of one micro-batch, each hot expert is picked by exactly 32 tokens. `cold_routes`: A token names 8 - 1 different cold experts; in each aligned block of 64 tokens of one micro-batch no cold expert is named more than 43 times.
All inputs are finite; a program needn't handle non-finite values.
Results may differ from a plain program's by a relative error of at most 0.0058.
Values may be sent and summed in bfloat16 or wider, within the bound.
A program may use at most 128 MiB of HBM per device.

v0:
```python
import functools

import jax
import jax.numpy as jnp
from jax import lax
from jax.experimental import pallas as pl
from jax.experimental.pallas import tpu as pltpu
from jax.sharding import PartitionSpec as P

TOP = 8
HOT = 2


def expert_rows(rows_in, weights):
    leading = rows_in.shape[:-1]
    flat_rows = rows_in.reshape(-1, rows_in.shape[-1])
    gate = jnp.dot(flat_rows, weights[0], preferred_element_type=jnp.float32)
    upward = jnp.dot(flat_rows, weights[1], preferred_element_type=jnp.float32)
    hidden = (jax.nn.silu(gate) * upward).astype(jnp.bfloat16)
    result = jnp.dot(hidden, weights[2], preferred_element_type=jnp.float32).astype(jnp.bfloat16)
    return result.reshape(leading + (result.shape[-1],))


def slot_table(routes_block, axis_width, capacity):
    expert = routes_block.reshape(-1)
    total_count = expert.shape[0]
    onehot = (expert[:, None] == jnp.arange(axis_width, dtype=jnp.int32)[None, :]).astype(jnp.int32)
    before = jnp.cumsum(onehot, axis=0) - onehot
    slot_rank = jnp.sum(before * onehot, axis=1)
    slot_place = expert * capacity + slot_rank
    target = jnp.arange(axis_width * capacity, dtype=jnp.int32)
    matched = slot_place[None, :] == target[:, None]
    filled = jnp.any(matched, axis=1)
    source = jnp.sum(
        jnp.where(matched, jnp.arange(total_count, dtype=jnp.int32)[None, :], 0), axis=1
    )
    return (slot_place, source, filled)


def routed(tokens, w_gate, w_up, w_down, hot_gate, hot_up, hot_down, cold_routes, hot_pick, gates):
    axis_width = lax.axis_size("expert")
    micro_count, local_tokens, model_width = tokens.shape
    picks = TOP - 1
    capacity = local_tokens * picks * 3 // (2 * axis_width) + 1
    own_weights = (w_gate[0], w_up[0], w_down[0])
    outbound = []
    tables = []
    for micro in range(micro_count):
        slot_place, source, filled = slot_table(cold_routes[micro], axis_width, capacity)
        rows_out = tokens[micro][source // picks]
        rows_out = jnp.where(filled[:, None], rows_out, jnp.zeros_like(rows_out))
        outbound.append(rows_out.reshape(axis_width, capacity, model_width))
        tables.append(slot_place)
    joined = jnp.concatenate(outbound, axis=1)
    back_all = lax.all_to_all(
        expert_rows(
            lax.all_to_all(joined, "expert", split_axis=0, concat_axis=0, tiled=True), own_weights
        ),
        "expert",
        split_axis=0,
        concat_axis=0,
        tiled=True,
    )
    returned = [
        back_all[:, micro * capacity : (micro + 1) * capacity] for micro in range(micro_count)
    ]
    cold_parts = []
    for micro in range(micro_count):
        picked = returned[micro].reshape(axis_width * capacity, model_width)[tables[micro]]
        picked = picked.reshape(local_tokens, picks, model_width).astype(jnp.float32)
        cold_parts.append(jnp.sum(picked * gates[micro, :, 1:, None], axis=1))
    cold_total = jnp.stack(cold_parts)
    all_rows = micro_count * local_tokens
    flat = tokens.reshape(all_rows, model_width)
    order = jnp.argsort(hot_pick.reshape(all_rows), stable=True)
    share = all_rows // HOT
    grouped = flat[order].reshape(HOT, share, model_width)
    gate = jnp.einsum(
        "hsd,hdf->hsf",
        grouped,
        lax.all_gather(hot_gate, "expert", axis=2, tiled=True),
        preferred_element_type=jnp.float32,
    )
    upward = jnp.einsum(
        "hsd,hdf->hsf",
        grouped,
        lax.all_gather(hot_up, "expert", axis=2, tiled=True),
        preferred_element_type=jnp.float32,
    )
    hidden = (jax.nn.silu(gate) * upward).astype(jnp.bfloat16)
    hot_sum = jnp.einsum(
        "hsf,hdf->hsd",
        hidden,
        lax.all_gather(hot_down, "expert", axis=2, tiled=True),
        preferred_element_type=jnp.float32,
    )
    sorted_out = hot_sum.astype(jnp.bfloat16).reshape(all_rows, model_width)
    inverse = jnp.argsort(order)
    hot_out = sorted_out[inverse].astype(jnp.float32) * gates[:, :, 0].reshape(all_rows)[:, None]
    total = hot_out.reshape(micro_count, local_tokens, model_width) + cold_total
    return total.astype(jnp.bfloat16)


QUARTERS = 4
ROOM = 56 * 2**20


def column(row):
    rows = row.shape[1]
    down = lax.broadcasted_iota(jnp.int32, (rows, rows), 0)
    across = lax.broadcasted_iota(jnp.int32, (rows, rows), 1)
    return jnp.sum(jnp.where(down == across, row, 0.0), axis=1, keepdims=True)


def fused(
    n, hot, part, tok, routes, pick, gts, wg_in, wu_in, wd_in, hg_in, hu_in, hd_in, out,
    xs, keep, sc, rc, sy, ry, sz, rz, wg, wu, wd, wh, hid, hhid, cs, ct,
    wsem, tsem, cts, ctr, up_s, down_s, z_r, y_s, y_r, c_s, c_r,
    rc_s, rc_r, ry_s, ry_r, rz_s, rz_r,
):
    nz = n // 4
    rows, model = tok.shape
    units = wg.shape[1]
    pad = hhid.shape[1]
    piece = rows // QUARTERS
    me = lax.axis_index("expert")
    c = lax.rem(me, 2)
    y = lax.rem(lax.div(me, 2), 2)
    z = lax.div(me, 4)
    own = y * 2 + c
    side = (1 - y) * 2 + c
    peer_y = z * 4 + side
    peer_c = z * 4 + y * 2 + (1 - c)

    def remote(src, dst, send, recv, device):
        return pltpu.make_async_remote_copy(
            src_ref=src, dst_ref=dst, send_sem=send, recv_sem=recv,
            device_id={"expert": device}, device_id_type=pl.DeviceIdType.MESH,
        )

    loads = [
        pltpu.make_async_copy(src, dst, wsem.at[i])
        for i, (src, dst) in enumerate((
            *(
                (src.at[h], wh.at[pl.ds(t * pad + h * part, part)])
                for t, src in enumerate((hg_in, hu_in, hd_in)) for h in range(hot)
            ),
            (wg_in, wg), (wu_in, wu), (wd_in, wd),
        ))
    ]
    first = pltpu.make_async_copy(tok, xs.at[z, own], tsem)
    first.start()
    for load in loads:
        load.start()

    barrier = pltpu.get_barrier_semaphore()

    @pl.loop(1, n)
    def _(i):
        pl.semaphore_signal(
            barrier, inc=1, device_id={"expert": lax.rem(me + i, n)},
            device_id_type=pl.DeviceIdType.MESH,
        )

    pl.semaphore_wait(barrier, n - 1)

    def ct_copy(i):
        peer = lax.rem(me + i, n)
        return remote(ct.at[peer], cs.at[me], cts.at[i], ctr.at[me], peer)

    def go_up(p):
        return remote(xs.at[p, own], xs.at[p, own], up_s.at[p], z_r.at[p], me + 4)

    def go_down(p):
        return remote(xs.at[p, own], xs.at[p, own], down_s.at[p], z_r.at[p], me - 4)

    def go_y(p):
        return remote(xs.at[p, own], xs.at[p, own], y_s.at[p], y_r.at[p], peer_y)

    def go_c(p, which):
        slot = own if which == 0 else side
        return remote(
            xs.at[p, slot], xs.at[p, slot], c_s.at[p, which], c_r.at[p, which], peer_c
        )

    def spread(p):
        @pl.when((p <= z) & (z + 1 < nz))
        def _():
            go_up(p).start()

        @pl.when((p >= z) & (z > 0))
        def _():
            go_down(p).start()

    def landed(p):
        remote(xs.at[p, own], xs.at[p, own], up_s.at[p], z_r.at[p], me).wait_recv()
        spread(p)
        go_y(p).start()
        go_c(p, 0).start()

    def plane(s):
        near = jnp.minimum(z, nz - 1 - z)
        step = lax.div(s + 1, 2)
        both = jnp.where(lax.rem(s, 2) == 1, z - step, z + step)
        far = jnp.where(z * 2 < nz, s, nz - 1 - s)
        return jnp.where(s <= 2 * near, both, far)

    def share(p, j, q):
        span = pl.ds(pl.multiple_of(q * piece, piece), piece)
        return remote(
            sc.at[p, j, span], rc.at[p, j, span], rc_s.at[p, j, q], rc_r.at[p, j, q], peer_c
        )

    def share_y(p, q):
        span = pl.ds(pl.multiple_of(q * piece, piece), piece)
        return remote(sy.at[p, span], ry.at[p, span], ry_s.at[p, q], ry_r.at[p, q], peer_y)

    def share_z(way, p, q):
        span = pl.ds(pl.multiple_of(q * piece, piece), piece)
        return remote(
            sz.at[way, p, span], rz.at[way, p, span], rz_s.at[way, p, q], rz_r.at[way, p, q],
            jnp.where(way == 0, me + 4, me - 4),
        )

    def compute(p):
        wide = 256 if units % 256 == 0 else units
        x = xs.at[p]
        cold_c = jnp.concatenate([column(cs[p * 4 + j, 0:1, :]) for j in range(4)], axis=0)

        @pl.loop(0, units // wide)
        def _(k):
            cols = pl.ds(pl.multiple_of(k * wide, wide), wide)
            v = x[...].reshape(4 * rows, model)
            g = jnp.dot(v, wg[:, cols], preferred_element_type=jnp.float32)
            u = jnp.dot(v, wu[:, cols], preferred_element_type=jnp.float32)
            hid[:, cols] = (g / (1.0 + jnp.exp(-g)) * u).astype(jnp.bfloat16)

        v = x[...].reshape(4 * rows, model)
        gu = lax.dot_general(
            v, wh[: 2 * pad, :], (((1,), (1,)), ((), ())), preferred_element_type=jnp.float32
        )
        g, u = gu[:, :pad], gu[:, pad:]
        lane = lax.broadcasted_iota(jnp.int32, (rows, pad), 1)
        warm = []
        for j in range(4):
            scale = jnp.zeros((rows, pad), jnp.float32)
            for h in range(hot):
                weight = column(cs[p * 4 + j, 1 + h : 2 + h, :])
                scale = jnp.where((lane >= h * part) & (lane < (h + 1) * part), weight, scale)
            warm.append(scale)
        warm = jnp.concatenate(warm, axis=0)
        hhid[...] = (g / (1.0 + jnp.exp(-g)) * u * warm).astype(jnp.bfloat16)

        tile = 512 if model % 512 == 0 else model

        @pl.loop(0, model // tile)
        def _(k):
            cols = pl.ds(pl.multiple_of(k * tile, tile), tile)
            r = jnp.dot(hid[...], wd[:, cols], preferred_element_type=jnp.float32)
            r = r.astype(jnp.bfloat16).astype(jnp.float32) * cold_c
            r = r + jnp.dot(hhid[...], wh[2 * pad :, cols], preferred_element_type=jnp.float32)
            for j in range(2):
                low = r[2 * j * rows : (2 * j + 1) * rows]
                high = r[(2 * j + 1) * rows : (2 * j + 2) * rows]
                keep[p, j, :, cols] = jnp.where(c == 0, low, high)
                sc[p, j, :, cols] = jnp.where(c == 0, high, low).astype(jnp.bfloat16)

    def y_step(p):
        @pl.loop(0, QUARTERS)
        def _(q):
            span = pl.ds(pl.multiple_of(q * piece, piece), piece)
            share(p, 1 - y, q).wait_recv()
            total = keep[p, 1 - y, span, :] + rc[p, 1 - y, span, :].astype(jnp.float32)
            sy[p, span, :] = total.astype(jnp.bfloat16)
            share_y(p, q).start()

        @pl.loop(0, QUARTERS)
        def _(q):
            span = pl.ds(pl.multiple_of(q * piece, piece), piece)
            share(p, y, q).wait_recv()
            keep[p, y, span, :] += rc[p, y, span, :].astype(jnp.float32)

    def z_step(k):
        @pl.loop(0, 2)
        def _(turn):
            way = jnp.where(z * 2 < nz, turn, 1 - turn)
            p = jnp.where(way == 0, k, nz - 1 - k)
            active = jnp.where(way == 0, z < k, z > nz - 1 - k)
            fed = jnp.where(way == 0, z > 0, z < nz - 1)

            @pl.when(active)
            def _():
                @pl.loop(0, QUARTERS)
                def _(q):
                    span = pl.ds(pl.multiple_of(q * piece, piece), piece)
                    share_y(p, q).wait_recv()
                    keep[p, y, span, :] += ry[p, span, :].astype(jnp.float32)

                    @pl.when(fed)
                    def _():
                        share_z(way, p, q).wait_recv()
                        keep[p, y, span, :] += rz[way, p, span, :].astype(jnp.float32)

                    sz[way, p, span, :] = keep[p, y, span, :].astype(jnp.bfloat16)
                    share_z(way, p, q).start()

    first.wait()
    spread(z)
    go_y(z).start()
    go_c(z, 0).start()

    if pad > hot * part:
        for t in range(3):
            blank = wh.at[pl.ds(t * pad + hot * part, pad - hot * part)]
            blank[...] = jnp.zeros_like(blank)

    ct[...] = jnp.zeros_like(ct)
    micros = gts.shape[0]

    def joined(parts):
        return jnp.concatenate(parts, axis=1)

    warm_row = joined([gts[m, 0:1, :] for m in range(micros)])
    chosen = joined([pick[m : m + 1, :] for m in range(micros)])
    named = [
        (
            joined([routes[k, m : m + 1, :] for m in range(micros)]),
            joined([gts[m, k + 1 : k + 2, :] for m in range(micros)]),
        )
        for k in range(routes.shape[0])
    ]

    def row(e):
        return sum(jnp.where(route == e, weight, 0.0) for route, weight in named)

    for e in range(n):
        ct[e, 0:1, :] = row(e)
        for h in range(hot):
            ct[e, 1 + h : 2 + h, :] = jnp.where(chosen == h, warm_row, 0.0)

    @pl.loop(1, n)
    def _(i):
        ct_copy(i).start()

    cs[me] = ct[me]

    @pl.loop(0, nz)
    def _(s):
        p = plane(s)

        @pl.when((s + 1 < nz) & (z - s - 1 >= 0))
        def _():
            landed(z - s - 1)

        @pl.when((s + 1 < nz) & (z + s + 1 < nz))
        def _():
            landed(z + s + 1)

        go_y(p).wait_recv()
        go_c(p, 1).start()

        @pl.when(s == 0)
        def _():
            for load in loads:
                load.wait()

            @pl.loop(1, n)
            def _(i):
                other = lax.rem(me + i, n)
                remote(ct.at[other], cs.at[other], cts.at[i], ctr.at[other], other).wait_recv()

        go_c(p, 0).wait_recv()
        go_c(p, 1).wait_recv()
        compute(p)

        @pl.loop(0, QUARTERS)
        def _(q):
            share(p, 1 - y, q).start()

        @pl.loop(0, QUARTERS)
        def _(q):
            share(p, y, q).start()

        @pl.when(s >= 1)
        def _():
            y_step(plane(s - 1))

        @pl.when(s >= 3)
        def _():
            z_step(s - 2)

    y_step(plane(nz - 1))
    for k in range(max(1, nz - 2), nz):
        z_step(k)

    @pl.loop(0, QUARTERS)
    def _(q):
        span = pl.ds(pl.multiple_of(q * piece, piece), piece)
        share_y(z, q).wait_recv()
        keep[z, y, span, :] += ry[z, span, :].astype(jnp.float32)

        @pl.when(z > 0)
        def _():
            share_z(0, z, q).wait_recv()
            keep[z, y, span, :] += rz[0, z, span, :].astype(jnp.float32)

        @pl.when(z < nz - 1)
        def _():
            share_z(1, z, q).wait_recv()
            keep[z, y, span, :] += rz[1, z, span, :].astype(jnp.float32)

        out[span, :] = keep[z, y, span, :].astype(jnp.bfloat16)

    @pl.loop(1, n)
    def _(i):
        ct_copy(i).wait_send()

    @pl.loop(0, nz)
    def _(p):
        @pl.when((p <= z) & (z + 1 < nz))
        def _():
            go_up(p).wait_send()

        @pl.when((p >= z) & (z > 0))
        def _():
            go_down(p).wait_send()

        go_y(p).wait_send()
        go_c(p, 0).wait_send()
        go_c(p, 1).wait_send()

        @pl.loop(0, QUARTERS)
        def _(q):
            share(p, 0, q).wait_send()
            share(p, 1, q).wait_send()
            share_y(p, q).wait_send()

            @pl.when(p > z)
            def _():
                share_z(0, p, q).wait_send()

            @pl.when(p < z)
            def _():
                share_z(1, p, q).wait_send()


def scratch(n, rows, model, units, pad, hot):
    nz = n // 4
    half, full = jnp.bfloat16, jnp.float32
    dma = pltpu.SemaphoreType.DMA
    return [
        pltpu.VMEM((nz, 4, rows, model), half),
        pltpu.VMEM((nz, 2, rows, model), full),
        pltpu.VMEM((nz, 2, rows, model), half),
        pltpu.VMEM((nz, 2, rows, model), half),
        pltpu.VMEM((nz, rows, model), half),
        pltpu.VMEM((nz, rows, model), half),
        pltpu.VMEM((2, nz, rows, model), half),
        pltpu.VMEM((2, nz, rows, model), half),
        pltpu.VMEM((model, units), half),
        pltpu.VMEM((model, units), half),
        pltpu.VMEM((units, model), half),
        pltpu.VMEM((3 * pad, model), half),
        pltpu.VMEM((4 * rows, units), half),
        pltpu.VMEM((4 * rows, pad), half),
        pltpu.VMEM((n, 8, rows), full),
        pltpu.VMEM((n, 8, rows), full),
        dma((3 + 3 * hot,)), dma, dma((n,)), dma((n,)),
        dma((nz,)), dma((nz,)), dma((nz,)), dma((nz,)), dma((nz,)), dma((nz, 2)), dma((nz, 2)),
        dma((nz, 2, QUARTERS)), dma((nz, 2, QUARTERS)),
        dma((nz, QUARTERS)), dma((nz, QUARTERS)),
        dma((2, nz, QUARTERS)), dma((2, nz, QUARTERS)),
    ]


def shards(tokens, w_gate, w_up, w_down, hot_gate, hot_up, hot_down, cold_routes, hot_pick, gates):
    n = lax.axis_size("expert")
    micro_count, local_tokens, model = tokens.shape
    rows = micro_count * local_tokens
    hot, units, part = hot_gate.shape[0], w_gate.shape[2], hot_gate.shape[2]
    pad = -(-hot * part // 128) * 128
    need = rows * model * n * 9 // 2 * 2 + 3 * model * (units + pad) * 2
    if n % 4 or part % 16 or rows % 64 or model % 256 or need > ROOM or hot > 7:
        return routed(
            tokens, w_gate, w_up, w_down, hot_gate, hot_up, hot_down, cold_routes, hot_pick, gates
        )
    anyplace = pl.BlockSpec(memory_space=pl.ANY)
    vmem = pl.BlockSpec(memory_space=pltpu.VMEM)
    mixed = pl.pallas_call(
        functools.partial(fused, n, hot, part),
        out_shape=jax.ShapeDtypeStruct((rows, model), jnp.bfloat16),
        in_specs=[anyplace, vmem, vmem, vmem] + [anyplace] * 6,
        out_specs=vmem,
        scratch_shapes=scratch(n, rows, model, units, pad, hot),
        compiler_params=pltpu.CompilerParams(
            collective_id=0, has_side_effects=True, vmem_limit_bytes=64 * 2**20 - 2**17
        ),
    )(
        tokens.reshape(rows, model), jnp.transpose(cold_routes, (2, 0, 1)), hot_pick,
        jnp.swapaxes(gates, 1, 2),
        w_gate[0], w_up[0], w_down[0],
        *(jnp.swapaxes(w, 1, 2) for w in (hot_gate, hot_up, hot_down)),
    )
    return mixed.reshape(tokens.shape)


def solution(mesh):
    in_specs = (
        P(None, ("groups", "expert"), None),
        P("expert", None, None),
        P("expert", None, None),
        P("expert", None, None),
        P(None, None, "expert"),
        P(None, None, "expert"),
        P(None, None, "expert"),
        P(None, ("groups", "expert"), None),
        P(None, ("groups", "expert")),
        P(None, ("groups", "expert"), None),
    )
    out_specs = P(None, ("groups", "expert"), None)
    return jax.shard_map(shards, mesh=mesh, in_specs=in_specs, out_specs=out_specs, check_vma=False)
```

profile of v0, /device:TPU:0, one launch (start us, length us, event | category | flops | bytes accessed | tf_op | source)
XLA Modules:
  0.0 129.9 jit_solution(17919266573299877713)
XLA Ops:
  0.0 128.0 %shard_map.100 = bf16[128,2048]{1,0:T(8,128)(2,1)} custom-call(bf16[128,2048]{1,0:T(8,128)(2,1)} %bitcast.14, s32[7,2,64]{2,1,0:T(2,128)} %bitcast.19, s32[2,64]{1,0:T(2,128)} %pick.1, f32[2,8,64]{2,1,0:T(8,128)} %bitcast.18, bf16[2048,768]{1,0:T(8,128)(2,1)} %bitcast.10, bf16[2048,768]{1,0:T(8,128)(2,1)} %bitcast.11, bf16[768,2048]{1,0:T(8,128)(2,1)} %bitcast.12, ...), custom_call_target="tpu_custom_call" | custom-call | tf_op jit(solution)/shard_map/pallas_call | solution.py:489
  128.0 1.9 %copy.12 = bf16[2,64,2048]{2,1,0:T(8,128)(2,1)} copy(bf16[2,64,2048]{2,1,0:T(8,128)(2,1)} %bitcast.13) | data formatting | bytes 1048576
where the time goes:
time: 130 us
  Pallas kernels  128 us (98%)
  local copies, waits for them, and re-layouts  1.88 us (1%)
    pallas_call x1, Pallas kernels, shards(): pl.pallas_call(functools.partial(fused, n, hot, part), out_shape=jax.Shap...  128 us

commit v1 on v0

--- a/solution.py
+++ b/solution.py
@@ -101,7 +101,9 @@
     return total.astype(jnp.bfloat16)
 
 
-QUARTERS = 4
+CHUNKS = 4
+GATHER_FAR = 3
+REDUCE_NEAR = 2
 ROOM = 56 * 2**20
 
 
@@ -110,6 +112,10 @@
     down = lax.broadcasted_iota(jnp.int32, (rows, rows), 0)
     across = lax.broadcasted_iota(jnp.int32, (rows, rows), 1)
     return jnp.sum(jnp.where(down == across, row, 0.0), axis=1, keepdims=True)
+
+
+def tile_of(extent, most):
+    return most if extent % most == 0 else extent
 
 
 def fused(
@@ -122,7 +128,10 @@
     rows, model = tok.shape
     units = wg.shape[1]
     pad = hhid.shape[1]
-    piece = rows // QUARTERS
+    piece = rows // CHUNKS
+    wide = tile_of(units, 256)
+    tile = tile_of(model, 512)
+    tiles = model // tile
     me = lax.axis_index("expert")
     c = lax.rem(me, 2)
     y = lax.rem(lax.div(me, 2), 2)
@@ -131,12 +140,16 @@
     side = (1 - y) * 2 + c
     peer_y = z * 4 + side
     peer_c = z * 4 + y * 2 + (1 - c)
+    corner = (z == 0) | (z == nz - 1)
 
     def remote(src, dst, send, recv, device):
         return pltpu.make_async_remote_copy(
             src_ref=src, dst_ref=dst, send_sem=send, recv_sem=recv,
             device_id={"expert": device}, device_id_type=pl.DeviceIdType.MESH,
         )
+
+    def span(k):
+        return pl.ds(pl.multiple_of(k * piece, piece), piece)
 
     loads = [
         pltpu.make_async_copy(src, dst, wsem.at[i])
@@ -162,41 +175,109 @@
             device_id_type=pl.DeviceIdType.MESH,
         )
 
+    if pad > hot * part:
+        for t in range(3):
+            blank = wh.at[pl.ds(t * pad + hot * part, pad - hot * part)]
+            blank[...] = jnp.zeros_like(blank)
+
+    ct[...] = jnp.zeros_like(ct)
+    micros = gts.shape[0]
+
+    def joined(parts):
+        return jnp.concatenate(parts, axis=1)
+
+    warm_row = joined([gts[m, 0:1, :] for m in range(micros)])
+    chosen = joined([pick[m : m + 1, :] for m in range(micros)])
+    named = [
+        (
+            joined([routes[k, m : m + 1, :] for m in range(micros)]),
+            joined([gts[m, k + 1 : k + 2, :] for m in range(micros)]),
+        )
+        for k in range(routes.shape[0])
+    ]
+
+    def row(e):
+        return sum(jnp.where(route == e, weight, 0.0) for route, weight in named)
+
+    for e in range(n):
+        ct[e, 0:1, :] = row(e)
+        for h in range(hot):
+            ct[e, 1 + h : 2 + h, :] = jnp.where(chosen == h, warm_row, 0.0)
+
+    cs[me] = ct[me]
     pl.semaphore_wait(barrier, n - 1)
 
     def ct_copy(i):
         peer = lax.rem(me + i, n)
         return remote(ct.at[peer], cs.at[me], cts.at[i], ctr.at[me], peer)
 
-    def go_up(p):
-        return remote(xs.at[p, own], xs.at[p, own], up_s.at[p], z_r.at[p], me + 4)
-
-    def go_down(p):
-        return remote(xs.at[p, own], xs.at[p, own], down_s.at[p], z_r.at[p], me - 4)
-
-    def go_y(p):
-        return remote(xs.at[p, own], xs.at[p, own], y_s.at[p], y_r.at[p], peer_y)
+    def go_own(p, k, send, device):
+        ref = xs.at[p, own, span(k)]
+        return remote(ref, ref, send.at[p, k], z_r.at[p, k], device)
+
+    def go_side(p, k, send, device):
+        ref = xs.at[p, side, span(k)]
+        at = CHUNKS + k - GATHER_FAR
+        return remote(ref, ref, send.at[p, at], z_r.at[p, at], device)
+
+    def go_y(p, k):
+        ref = xs.at[p, own, span(k)]
+        return remote(ref, ref, y_s.at[p, k], y_r.at[p, k], peer_y)
 
     def go_c(p, which):
-        slot = own if which == 0 else side
-        return remote(
-            xs.at[p, slot], xs.at[p, slot], c_s.at[p, which], c_r.at[p, which], peer_c
-        )
-
-    def spread(p):
+        ref = xs.at[p, own if which == 0 else side]
+        return remote(ref, ref, c_s.at[p, which], c_r.at[p, which], peer_c)
+
+    def relay(p, k, go):
         @pl.when((p <= z) & (z + 1 < nz))
         def _():
-            go_up(p).start()
+            go(p, k, up_s, me + 4).start()
 
         @pl.when((p >= z) & (z > 0))
         def _():
-            go_down(p).start()
-
-    def landed(p):
-        remote(xs.at[p, own], xs.at[p, own], up_s.at[p], z_r.at[p], me).wait_recv()
-        spread(p)
-        go_y(p).start()
-        go_c(p, 0).start()
+            go(p, k, down_s, me - 4).start()
+
+    def at_distance(d, act):
+        @pl.when(z - d >= 0)
+        def _():
+            act(z - d)
+
+        @pl.when(z + d < nz)
+        def _():
+            act(z + d)
+
+    def serve_own(d, k):
+        def act(p):
+            go_own(p, k, up_s, me).wait_recv()
+            relay(p, k, go_own)
+
+            @pl.when(k < GATHER_FAR)
+            def _():
+                go_y(p, k).start()
+
+            @pl.when(k == CHUNKS - 1)
+            def _():
+                go_c(p, 0).start()
+
+        at_distance(d, act)
+
+    def serve_side(d):
+        def act(p):
+            @pl.loop(GATHER_FAR, CHUNKS)
+            def _(k):
+                go_side(p, k, up_s, me).wait_recv()
+                relay(p, k, go_side)
+
+        at_distance(d, act)
+
+    def ready(p):
+        @pl.loop(0, GATHER_FAR)
+        def _(k):
+            go_y(p, k).wait_recv()
+
+        go_c(p, 1).start()
+        go_c(p, 0).wait_recv()
+        go_c(p, 1).wait_recv()
 
     def plane(s):
         near = jnp.minimum(z, nz - 1 - z)
@@ -205,25 +286,33 @@
         far = jnp.where(z * 2 < nz, s, nz - 1 - s)
         return jnp.where(s <= 2 * near, both, far)
 
-    def share(p, j, q):
-        span = pl.ds(pl.multiple_of(q * piece, piece), piece)
+    def share(p, j, t):
+        cols = pl.ds(pl.multiple_of(t * tile, tile), tile)
         return remote(
-            sc.at[p, j, span], rc.at[p, j, span], rc_s.at[p, j, q], rc_r.at[p, j, q], peer_c
-        )
-
-    def share_y(p, q):
-        span = pl.ds(pl.multiple_of(q * piece, piece), piece)
-        return remote(sy.at[p, span], ry.at[p, span], ry_s.at[p, q], ry_r.at[p, q], peer_y)
-
-    def share_z(way, p, q):
-        span = pl.ds(pl.multiple_of(q * piece, piece), piece)
+            sc.at[p, j, :, cols], rc.at[p, j, :, cols], rc_s.at[p, j, t], rc_r.at[p, j, t], peer_c
+        )
+
+    def share_y(p, k):
         return remote(
-            sz.at[way, p, span], rz.at[way, p, span], rz_s.at[way, p, q], rz_r.at[way, p, q],
+            sy.at[p, span(k)], ry.at[p, span(k)], ry_s.at[p, k], ry_r.at[p, k], peer_y
+        )
+
+    def share_z(way, p, at):
+        landing = jnp.where((way == 1) & (z - 1 == p), nz, p)
+        return remote(
+            sz.at[p, span(at)], rz.at[landing, span(at)], rz_s.at[p, at], rz_r.at[landing, at],
             jnp.where(way == 0, me + 4, me - 4),
         )
 
-    def compute(p):
-        wide = 256 if units % 256 == 0 else units
+    def land_z(slot, at):
+        return remote(
+            rz.at[slot, span(at)], rz.at[slot, span(at)], rz_s.at[0, at], rz_r.at[slot, at], me
+        )
+
+    hooks = units // wide + 1
+    per = -(-CHUNKS // hooks)
+
+    def compute(p, hook, middle):
         x = xs.at[p]
         cold_c = jnp.concatenate([column(cs[p * 4 + j, 0:1, :]) for j in range(4)], axis=0)
 
@@ -234,6 +323,7 @@
             g = jnp.dot(v, wg[:, cols], preferred_element_type=jnp.float32)
             u = jnp.dot(v, wu[:, cols], preferred_element_type=jnp.float32)
             hid[:, cols] = (g / (1.0 + jnp.exp(-g)) * u).astype(jnp.bfloat16)
+            hook(k)
 
         v = x[...].reshape(4 * rows, model)
         gu = lax.dot_general(
@@ -250,12 +340,12 @@
             warm.append(scale)
         warm = jnp.concatenate(warm, axis=0)
         hhid[...] = (g / (1.0 + jnp.exp(-g)) * u * warm).astype(jnp.bfloat16)
-
-        tile = 512 if model % 512 == 0 else model
-
-        @pl.loop(0, model // tile)
-        def _(k):
-            cols = pl.ds(pl.multiple_of(k * tile, tile), tile)
+        hook(hooks - 1)
+        middle()
+
+        @pl.loop(0, tiles)
+        def _(t):
+            cols = pl.ds(pl.multiple_of(t * tile, tile), tile)
             r = jnp.dot(hid[...], wd[:, cols], preferred_element_type=jnp.float32)
             r = r.astype(jnp.bfloat16).astype(jnp.float32) * cold_c
             r = r + jnp.dot(hhid[...], wh[2 * pad :, cols], preferred_element_type=jnp.float32)
@@ -264,152 +354,187 @@
                 high = r[(2 * j + 1) * rows : (2 * j + 2) * rows]
                 keep[p, j, :, cols] = jnp.where(c == 0, low, high)
                 sc[p, j, :, cols] = jnp.where(c == 0, high, low).astype(jnp.bfloat16)
-
-    def y_step(p):
-        @pl.loop(0, QUARTERS)
-        def _(q):
-            span = pl.ds(pl.multiple_of(q * piece, piece), piece)
-            share(p, 1 - y, q).wait_recv()
-            total = keep[p, 1 - y, span, :] + rc[p, 1 - y, span, :].astype(jnp.float32)
-            sy[p, span, :] = total.astype(jnp.bfloat16)
-            share_y(p, q).start()
-
-        @pl.loop(0, QUARTERS)
-        def _(q):
-            span = pl.ds(pl.multiple_of(q * piece, piece), piece)
-            share(p, y, q).wait_recv()
-            keep[p, y, span, :] += rc[p, y, span, :].astype(jnp.float32)
-
-    def z_step(k):
-        @pl.loop(0, 2)
-        def _(turn):
-            way = jnp.where(z * 2 < nz, turn, 1 - turn)
-            p = jnp.where(way == 0, k, nz - 1 - k)
-            active = jnp.where(way == 0, z < k, z > nz - 1 - k)
-            fed = jnp.where(way == 0, z > 0, z < nz - 1)
-
-            @pl.when(active)
-            def _():
-                @pl.loop(0, QUARTERS)
-                def _(q):
-                    span = pl.ds(pl.multiple_of(q * piece, piece), piece)
-                    share_y(p, q).wait_recv()
-                    keep[p, y, span, :] += ry[p, span, :].astype(jnp.float32)
-
-                    @pl.when(fed)
-                    def _():
-                        share_z(way, p, q).wait_recv()
-                        keep[p, y, span, :] += rz[way, p, span, :].astype(jnp.float32)
-
-                    sz[way, p, span, :] = keep[p, y, span, :].astype(jnp.bfloat16)
-                    share_z(way, p, q).start()
+            share(p, 0, t).start()
+            share(p, 1, t).start()
+
+    def both_cores(p, j, k):
+        return keep[p, j, span(k), :] + rc[p, j, span(k), :].astype(jnp.float32)
+
+    def cross(p):
+        @pl.loop(0, tiles)
+        def _(t):
+            share(p, 0, t).wait_recv()
+            share(p, 1, t).wait_recv()
+
+        @pl.loop(0, REDUCE_NEAR)
+        def _(k):
+            sy[p, span(k), :] = both_cores(p, 1 - y, k).astype(jnp.bfloat16)
+            share_y(p, k).start()
+
+    def onward(way, p, fed, at, total):
+        value = total()
+        if fed:
+            land_z(p, at).wait_recv()
+            value = value + rz[p, span(at), :].astype(jnp.float32)
+        sz[p, span(at), :] = value.astype(jnp.bfloat16)
+        share_z(way, p, at).start()
+
+    def far_side(way, p, fed, k):
+        onward(way, p, fed, CHUNKS + k - REDUCE_NEAR, lambda: both_cores(p, 1 - y, k))
+
+    def far_own(way, p, fed, k):
+        onward(way, p, fed, k, lambda: both_cores(p, y, k))
+
+    def near_own(way, p, fed, k):
+        share_y(p, k).wait_recv()
+        onward(
+            way, p, fed, k,
+            lambda: both_cores(p, y, k) + ry[p, span(k), :].astype(jnp.float32),
+        )
+
+    out_way = jnp.where(z == 0, 0, 1)
+
+    def send_far(p):
+        @pl.loop(REDUCE_NEAR, CHUNKS)
+        def _(k):
+            far_side(out_way, p, False, k)
+            far_own(out_way, p, False, k)
+
+    def send_near(p):
+        @pl.loop(0, REDUCE_NEAR)
+        def _(k):
+            near_own(out_way, p, False, k)
+
+    def forward(hop):
+        def ways(act):
+            @pl.loop(0, 2)
+            def _(turn):
+                way = jnp.where(z * 2 < nz, turn, 1 - turn)
+                p = jnp.where(way == 0, hop, nz - 1 - hop)
+                active = jnp.where(way == 0, z < hop, z > nz - 1 - hop)
+
+                @pl.when(active)
+                def _():
+                    act(way, p)
+
+        @pl.loop(REDUCE_NEAR, CHUNKS)
+        def _(k):
+            def act(way, p):
+                far_side(way, p, True, k)
+                far_own(way, p, True, k)
+            ways(act)
+
+        @pl.loop(0, REDUCE_NEAR)
+        def _(k):
+            ways(lambda way, p: near_own(way, p, True, k))
+
+    def arrived(j, k, at):
+        keep[z, j, span(k), :] = both_cores(z, j, k)
+
+        @pl.when(z > 0)
+        def _():
+            land_z(z, at).wait_recv()
+            keep[z, j, span(k), :] += rz[z, span(at), :].astype(jnp.float32)
+
+        @pl.when(z < nz - 1)
+        def _():
+            land_z(nz, at).wait_recv()
+            keep[z, j, span(k), :] += rz[nz, span(at), :].astype(jnp.float32)
+
+    def finish_side():
+        @pl.loop(REDUCE_NEAR, CHUNKS)
+        def _(k):
+            arrived(1 - y, k, CHUNKS + k - REDUCE_NEAR)
+            sy[z, span(k), :] = keep[z, 1 - y, span(k), :].astype(jnp.bfloat16)
+            share_y(z, k).start()
+
+    def finish_own(low, high):
+        @pl.loop(low, high)
+        def _(k):
+            arrived(y, k, k)
+            share_y(z, k).wait_recv()
+            out[span(k), :] = (
+                keep[z, y, span(k), :] + ry[z, span(k), :].astype(jnp.float32)
+            ).astype(jnp.bfloat16)
 
     first.wait()
-    spread(z)
-    go_y(z).start()
+
+    @pl.loop(GATHER_FAR, CHUNKS)
+    def _(k):
+        go_y(z, k).start()
+
+    @pl.loop(0, CHUNKS)
+    def _(k):
+        relay(z, k, go_own)
+
+    @pl.loop(0, GATHER_FAR)
+    def _(k):
+        go_y(z, k).start()
+
     go_c(z, 0).start()
-
-    if pad > hot * part:
-        for t in range(3):
-            blank = wh.at[pl.ds(t * pad + hot * part, pad - hot * part)]
-            blank[...] = jnp.zeros_like(blank)
-
-    ct[...] = jnp.zeros_like(ct)
-    micros = gts.shape[0]
-
-    def joined(parts):
-        return jnp.concatenate(parts, axis=1)
-
-    warm_row = joined([gts[m, 0:1, :] for m in range(micros)])
-    chosen = joined([pick[m : m + 1, :] for m in range(micros)])
-    named = [
-        (
-            joined([routes[k, m : m + 1, :] for m in range(micros)]),
-            joined([gts[m, k + 1 : k + 2, :] for m in range(micros)]),
-        )
-        for k in range(routes.shape[0])
-    ]
-
-    def row(e):
-        return sum(jnp.where(route == e, weight, 0.0) for route, weight in named)
-
-    for e in range(n):
-        ct[e, 0:1, :] = row(e)
-        for h in range(hot):
-            ct[e, 1 + h : 2 + h, :] = jnp.where(chosen == h, warm_row, 0.0)
 
     @pl.loop(1, n)
     def _(i):
         ct_copy(i).start()
 
-    cs[me] = ct[me]
-
-    @pl.loop(0, nz)
+    @pl.loop(GATHER_FAR, CHUNKS)
+    def _(k):
+        go_y(z, k).wait_recv()
+        relay(z, k, go_side)
+
+    @pl.loop(0, CHUNKS)
+    def _(k):
+        serve_own(1, k)
+
+    for load in loads:
+        load.wait()
+
+    @pl.loop(1, n)
+    def _(i):
+        other = lax.rem(me + i, n)
+        remote(ct.at[other], cs.at[other], cts.at[i], ctr.at[other], other).wait_recv()
+
+    ready(z)
+    compute(z, lambda i: None, lambda: serve_side(1))
+    cross(z)
+
+    @pl.loop(1, nz)
     def _(s):
         p = plane(s)
-
-        @pl.when((s + 1 < nz) & (z - s - 1 >= 0))
-        def _():
-            landed(z - s - 1)
-
-        @pl.when((s + 1 < nz) & (z + s + 1 < nz))
-        def _():
-            landed(z + s + 1)
-
-        go_y(p).wait_recv()
-        go_c(p, 1).start()
-
-        @pl.when(s == 0)
-        def _():
-            for load in loads:
-                load.wait()
-
-            @pl.loop(1, n)
-            def _(i):
-                other = lax.rem(me + i, n)
-                remote(ct.at[other], cs.at[other], cts.at[i], ctr.at[other], other).wait_recv()
-
-        go_c(p, 0).wait_recv()
-        go_c(p, 1).wait_recv()
-        compute(p)
-
-        @pl.loop(0, QUARTERS)
-        def _(q):
-            share(p, 1 - y, q).start()
-
-        @pl.loop(0, QUARTERS)
-        def _(q):
-            share(p, y, q).start()
-
-        @pl.when(s >= 1)
-        def _():
-            y_step(plane(s - 1))
-
-        @pl.when(s >= 3)
-        def _():
-            z_step(s - 2)
-
-    y_step(plane(nz - 1))
-    for k in range(max(1, nz - 2), nz):
-        z_step(k)
-
-    @pl.loop(0, QUARTERS)
-    def _(q):
-        span = pl.ds(pl.multiple_of(q * piece, piece), piece)
-        share_y(z, q).wait_recv()
-        keep[z, y, span, :] += ry[z, span, :].astype(jnp.float32)
-
-        @pl.when(z > 0)
-        def _():
-            share_z(0, z, q).wait_recv()
-            keep[z, y, span, :] += rz[0, z, span, :].astype(jnp.float32)
-
-        @pl.when(z < nz - 1)
-        def _():
-            share_z(1, z, q).wait_recv()
-            keep[z, y, span, :] += rz[1, z, span, :].astype(jnp.float32)
-
-        out[span, :] = keep[z, y, span, :].astype(jnp.bfloat16)
+        ready(p)
+
+        def hook(i):
+            @pl.loop(i * per, jnp.minimum(CHUNKS, (i + 1) * per))
+            def _(k):
+                serve_own(s + 1, k)
+
+        def middle():
+            serve_side(s + 1)
+
+            @pl.when(corner & (s >= 2))
+            def _():
+                send_near(plane(s - 1))
+
+        compute(p, hook, middle)
+        cross(p)
+
+        @pl.when(corner)
+        def _():
+            send_far(p)
+
+    @pl.when(corner)
+    def _():
+        send_near(plane(nz - 1))
+        finish_side()
+
+    @pl.when(jnp.logical_not(corner))
+    def _():
+        for hop in range(2, nz):
+            if hop == nz - 1:
+                finish_side()
+            forward(hop)
+
+    finish_own(0, CHUNKS)
 
     @pl.loop(1, n)
     def _(i):
@@ -417,37 +542,53 @@
 
     @pl.loop(0, nz)
     def _(p):
-        @pl.when((p <= z) & (z + 1 < nz))
-        def _():
-            go_up(p).wait_send()
-
-        @pl.when((p >= z) & (z > 0))
-        def _():
-            go_down(p).wait_send()
-
-        go_y(p).wait_send()
+        def sent(k, go):
+            @pl.when((p <= z) & (z + 1 < nz))
+            def _():
+                go(p, k, up_s, me + 4).wait_send()
+
+            @pl.when((p >= z) & (z > 0))
+            def _():
+                go(p, k, down_s, me - 4).wait_send()
+
+        @pl.loop(0, CHUNKS)
+        def _(k):
+            sent(k, go_own)
+
+            @pl.when((k < GATHER_FAR) | (p == z))
+            def _():
+                go_y(p, k).wait_send()
+
+            @pl.when(k >= GATHER_FAR)
+            def _():
+                sent(k, go_side)
+
+            @pl.when((k < REDUCE_NEAR) | (p == z))
+            def _():
+                share_y(p, k).wait_send()
+
         go_c(p, 0).wait_send()
         go_c(p, 1).wait_send()
 
-        @pl.loop(0, QUARTERS)
-        def _(q):
-            share(p, 0, q).wait_send()
-            share(p, 1, q).wait_send()
-            share_y(p, q).wait_send()
-
-            @pl.when(p > z)
-            def _():
-                share_z(0, p, q).wait_send()
-
-            @pl.when(p < z)
-            def _():
-                share_z(1, p, q).wait_send()
+        @pl.loop(0, tiles)
+        def _(t):
+            share(p, 0, t).wait_send()
+            share(p, 1, t).wait_send()
+
+        @pl.when(p != z)
+        def _():
+            @pl.loop(0, 2 * CHUNKS - REDUCE_NEAR)
+            def _(at):
+                share_z(jnp.where(p > z, 0, 1), p, at).wait_send()
 
 
 def scratch(n, rows, model, units, pad, hot):
     nz = n // 4
     half, full = jnp.bfloat16, jnp.float32
     dma = pltpu.SemaphoreType.DMA
+    piece = rows // CHUNKS
+    gathers, reduces = 2 * CHUNKS - GATHER_FAR, 2 * CHUNKS - REDUCE_NEAR
+    tiles = model // tile_of(model, 512)
     return [
         pltpu.VMEM((nz, 4, rows, model), half),
         pltpu.VMEM((nz, 2, rows, model), full),
@@ -455,8 +596,8 @@
         pltpu.VMEM((nz, 2, rows, model), half),
         pltpu.VMEM((nz, rows, model), half),
         pltpu.VMEM((nz, rows, model), half),
-        pltpu.VMEM((2, nz, rows, model), half),
-        pltpu.VMEM((2, nz, rows, model), half),
+        pltpu.VMEM((nz, reduces * piece, model), half),
+        pltpu.VMEM((nz + 1, reduces * piece, model), half),
         pltpu.VMEM((model, units), half),
         pltpu.VMEM((model, units), half),
         pltpu.VMEM((units, model), half),
@@ -466,10 +607,11 @@
         pltpu.VMEM((n, 8, rows), full),
         pltpu.VMEM((n, 8, rows), full),
         dma((3 + 3 * hot,)), dma, dma((n,)), dma((n,)),
-        dma((nz,)), dma((nz,)), dma((nz,)), dma((nz,)), dma((nz,)), dma((nz, 2)), dma((nz, 2)),
-        dma((nz, 2, QUARTERS)), dma((nz, 2, QUARTERS)),
-        dma((nz, QUARTERS)), dma((nz, QUARTERS)),
-        dma((2, nz, QUARTERS)), dma((2, nz, QUARTERS)),
+        dma((nz, gathers)), dma((nz, gathers)), dma((nz, gathers)),
+        dma((nz, CHUNKS)), dma((nz, CHUNKS)), dma((nz, 2)), dma((nz, 2)),
+        dma((nz, 2, tiles)), dma((nz, 2, tiles)),
+        dma((nz, CHUNKS)), dma((nz, CHUNKS)),
+        dma((nz, reduces)), dma((nz + 1, reduces)),
     ]
 
 

time: 130 us -> 119 us (0.915)
  Pallas kernels: 128 us -> 117 us
    pallas_call x1, Pallas kernels: 128 us -> 117 us  [shards(): pl.pallas_call(functools.partial(fused, n, hot, part), out_shape=jax.Shap...]
where the time goes in v1:
time: 119 us
  Pallas kernels  117 us (98%)
  local copies, waits for them, and re-layouts  1.88 us (2%)
    pallas_call x1, Pallas kernels, shards(): pl.pallas_call(functools.partial(fused, n, hot, part), out_shape=jax.Shap...  117 us

profile of v1, /device:TPU:0, one launch (start us, length us, event | category | flops | bytes accessed | tf_op | source)
XLA Modules:
  0.0 118.7 jit_solution(1058779610197989699)
XLA Ops:
  0.0 116.8 %shard_map.100 = bf16[128,2048]{1,0:T(8,128)(2,1)} custom-call(bf16[128,2048]{1,0:T(8,128)(2,1)} %bitcast.14, s32[7,2,64]{2,1,0:T(2,128)} %bitcast.19, s32[2,64]{1,0:T(2,128)} %pick.1, f32[2,8,64]{2,1,0:T(8,128)} %bitcast.18, bf16[2048,768]{1,0:T(8,128)(2,1)} %bitcast.10, bf16[2048,768]{1,0:T(8,128)(2,1)} %bitcast.11, bf16[768,2048]{1,0:T(8,128)(2,1)} %bitcast.12, ...), custom_call_target="tpu_custom_call" | custom-call | tf_op jit(solution)/shard_map/pallas_call | solution.py:631
  116.8 1.9 %copy.12 = bf16[2,64,2048]{2,1,0:T(8,128)(2,1)} copy(bf16[2,64,2048]{2,1,0:T(8,128)(2,1)} %bitcast.13) | data formatting | bytes 1048576

commit v2 on v0

v2 whole, which is shorter than its diff:
```python
import functools

import jax
import jax.numpy as jnp
from jax import lax
from jax.experimental import pallas as pl
from jax.experimental.pallas import tpu as pltpu
from jax.sharding import PartitionSpec as P

TOP = 8
HOT = 2


def expert_rows(rows_in, weights):
    leading = rows_in.shape[:-1]
    flat_rows = rows_in.reshape(-1, rows_in.shape[-1])
    gate = jnp.dot(flat_rows, weights[0], preferred_element_type=jnp.float32)
    upward = jnp.dot(flat_rows, weights[1], preferred_element_type=jnp.float32)
    hidden = (jax.nn.silu(gate) * upward).astype(jnp.bfloat16)
    result = jnp.dot(hidden, weights[2], preferred_element_type=jnp.float32).astype(jnp.bfloat16)
    return result.reshape(leading + (result.shape[-1],))


def slot_table(routes_block, axis_width, capacity):
    expert = routes_block.reshape(-1)
    total_count = expert.shape[0]
    onehot = (expert[:, None] == jnp.arange(axis_width, dtype=jnp.int32)[None, :]).astype(jnp.int32)
    before = jnp.cumsum(onehot, axis=0) - onehot
    slot_rank = jnp.sum(before * onehot, axis=1)
    slot_place = expert * capacity + slot_rank
    target = jnp.arange(axis_width * capacity, dtype=jnp.int32)
    matched = slot_place[None, :] == target[:, None]
    filled = jnp.any(matched, axis=1)
    source = jnp.sum(
        jnp.where(matched, jnp.arange(total_count, dtype=jnp.int32)[None, :], 0), axis=1
    )
    return (slot_place, source, filled)


def routed(tokens, w_gate, w_up, w_down, hot_gate, hot_up, hot_down, cold_routes, hot_pick, gates):
    axis_width = lax.axis_size("expert")
    micro_count, local_tokens, model_width = tokens.shape
    picks = TOP - 1
    capacity = local_tokens * picks * 3 // (2 * axis_width) + 1
    own_weights = (w_gate[0], w_up[0], w_down[0])
    outbound = []
    tables = []
    for micro in range(micro_count):
        slot_place, source, filled = slot_table(cold_routes[micro], axis_width, capacity)
        rows_out = tokens[micro][source // picks]
        rows_out = jnp.where(filled[:, None], rows_out, jnp.zeros_like(rows_out))
        outbound.append(rows_out.reshape(axis_width, capacity, model_width))
        tables.append(slot_place)
    joined = jnp.concatenate(outbound, axis=1)
    back_all = lax.all_to_all(
        expert_rows(
            lax.all_to_all(joined, "expert", split_axis=0, concat_axis=0, tiled=True), own_weights
        ),
        "expert",
        split_axis=0,
        concat_axis=0,
        tiled=True,
    )
    returned = [
        back_all[:, micro * capacity : (micro + 1) * capacity] for micro in range(micro_count)
    ]
    cold_parts = []
    for micro in range(micro_count):
        picked = returned[micro].reshape(axis_width * capacity, model_width)[tables[micro]]
        picked = picked.reshape(local_tokens, picks, model_width).astype(jnp.float32)
        cold_parts.append(jnp.sum(picked * gates[micro, :, 1:, None], axis=1))
    cold_total = jnp.stack(cold_parts)
    all_rows = micro_count * local_tokens
    flat = tokens.reshape(all_rows, model_width)
    order = jnp.argsort(hot_pick.reshape(all_rows), stable=True)
    share = all_rows // HOT
    grouped = flat[order].reshape(HOT, share, model_width)
    gate = jnp.einsum(
        "hsd,hdf->hsf",
        grouped,
        lax.all_gather(hot_gate, "expert", axis=2, tiled=True),
        preferred_element_type=jnp.float32,
    )
    upward = jnp.einsum(
        "hsd,hdf->hsf",
        grouped,
        lax.all_gather(hot_up, "expert", axis=2, tiled=True),
        preferred_element_type=jnp.float32,
    )
    hidden = (jax.nn.silu(gate) * upward).astype(jnp.bfloat16)
    hot_sum = jnp.einsum(
        "hsf,hdf->hsd",
        hidden,
        lax.all_gather(hot_down, "expert", axis=2, tiled=True),
        preferred_element_type=jnp.float32,
    )
    sorted_out = hot_sum.astype(jnp.bfloat16).reshape(all_rows, model_width)
    inverse = jnp.argsort(order)
    hot_out = sorted_out[inverse].astype(jnp.float32) * gates[:, :, 0].reshape(all_rows)[:, None]
    total = hot_out.reshape(micro_count, local_tokens, model_width) + cold_total
    return total.astype(jnp.bfloat16)


(
    CROSS_FIRST, SEND_Z, SEND_Y, SEND_CORE, PASS_Z, PASS_CORE, RELAY_OWN, RELAY_SIDE,
    RELAY_CORE, CROSS, REDUCE_SIDE, REDUCE_FAR, REDUCE_NEAR, FINISH_SIDE, FINISH_OWN, STEP,
) = range(16)
OWN, SIDE, FROM_Y, CORE_OWN, CORE_SIDE, SHARE_OWN, SHARE_SIDE, SUM_Y, SUM_Z = range(9)
AHEAD, BEHIND = range(2)
CHUNKS = 8
NEAR_IN = 7
NEAR_OUT = 4
HIGH = (5, 4, 6, 7)
LOW = (3, 2, 0, 1)
STEPS = 6
UNITS = (
    ((2, 0), (1, 0), (3, 0), (0, 1), (3, 1), (2, 1), (1, 1), (0, 0)),
    ((0, 0), (1, 1), (2, 0), (0, 1), (1, 0), (3, 0), (3, 1), (2, 1)),
)
OUTER = (
    (SEND_Z, 6, AHEAD), (SEND_CORE,), (SEND_Y, 6), (CROSS_FIRST,), (SEND_Z, 7, AHEAD),
    (SEND_Z, 4, AHEAD), (SEND_Y, 2), (RELAY_OWN, 1, 5), (SEND_Y, 1), (SEND_Z, 5, AHEAD),
    (PASS_CORE, 6), (SEND_Z, 2, AHEAD), (SEND_Z, 1, AHEAD), (PASS_Z, 7), (SEND_Z, 3, AHEAD),
    (PASS_CORE, 7), (RELAY_OWN, 1, 4), (PASS_CORE, 2), (RELAY_OWN, 2, 7), (RELAY_CORE, 1, 5),
    (RELAY_OWN, 2, 4), (PASS_CORE, 1), (RELAY_SIDE, 1, 7), (RELAY_CORE, 1, 4), (RELAY_OWN, 2, 5),
    (SEND_Z, 0, AHEAD), (RELAY_CORE, 2, 4), (RELAY_OWN, 2, 6), (SEND_Y, 0), (RELAY_SIDE, 2, 7),
    (RELAY_CORE, 2, 5), (RELAY_OWN, 3, 7), (RELAY_CORE, 2, 6), (STEP, 0, 0), (RELAY_OWN, 2, 0),
    (PASS_CORE, 0), (RELAY_OWN, 1, 6), (STEP, 0, 1), (STEP, 0, 2), (RELAY_OWN, 3, 4),
    (STEP, 0, 3), (STEP, 0, 4), (RELAY_OWN, 3, 6), (STEP, 0, 5), (RELAY_CORE, 2, 0),
    (RELAY_CORE, 1, 6), (SEND_Y, 5), (RELAY_OWN, 3, 5), (RELAY_OWN, 1, 0), (REDUCE_FAR, 2, 4),
    (REDUCE_FAR, 2, 6), (REDUCE_FAR, 2, 5), (REDUCE_FAR, 2, 7), (REDUCE_SIDE, 2, 7),
    (REDUCE_SIDE, 2, 5), (REDUCE_SIDE, 2, 4), (RELAY_CORE, 3, 4), (REDUCE_SIDE, 2, 6),
    (RELAY_OWN, 1, 7), (RELAY_CORE, 3, 6), (STEP, 1, 0), (RELAY_OWN, 2, 3), (STEP, 1, 1),
    (PASS_CORE, 5), (RELAY_OWN, 3, 1), (STEP, 1, 2), (RELAY_CORE, 3, 5), (RELAY_SIDE, 3, 7),
    (STEP, 1, 3), (STEP, 1, 4), (RELAY_CORE, 1, 0), (SEND_Y, 3), (RELAY_OWN, 3, 3), (STEP, 1, 5),
    (STEP, 2, 0), (RELAY_CORE, 2, 3), (RELAY_OWN, 2, 1), (REDUCE_FAR, 1, 6), (STEP, 2, 1),
    (RELAY_OWN, 1, 1), (RELAY_CORE, 3, 1), (REDUCE_SIDE, 1, 6), (STEP, 2, 2), (PASS_CORE, 3),
    (STEP, 2, 3), (STEP, 2, 4), (RELAY_CORE, 3, 3), (STEP, 2, 5), (RELAY_OWN, 3, 2), (STEP, 3, 0),
    (RELAY_OWN, 3, 0), (REDUCE_FAR, 3, 6), (REDUCE_FAR, 3, 5), (RELAY_CORE, 2, 1),
    (REDUCE_FAR, 3, 4), (REDUCE_SIDE, 3, 7), (REDUCE_SIDE, 3, 6), (REDUCE_SIDE, 3, 4),
    (STEP, 3, 1), (RELAY_OWN, 1, 3), (RELAY_CORE, 1, 1), (STEP, 3, 2), (RELAY_OWN, 2, 2),
    (SEND_Y, 4), (STEP, 3, 3), (STEP, 3, 4), (RELAY_CORE, 3, 0), (STEP, 3, 5), (REDUCE_FAR, 1, 4),
    (RELAY_OWN, 1, 2), (REDUCE_FAR, 1, 5), (RELAY_CORE, 1, 3), (REDUCE_SIDE, 1, 5),
    (REDUCE_FAR, 1, 7), (REDUCE_SIDE, 1, 7), (REDUCE_SIDE, 1, 4), (REDUCE_SIDE, 3, 5),
    (REDUCE_FAR, 3, 7), (RELAY_CORE, 3, 2), (CROSS, 0, 3), (CROSS, 0, 1), (CROSS, 0, 0),
    (CROSS, 0, 2), (RELAY_CORE, 2, 2), (STEP, 4, 0), (STEP, 4, 1), (STEP, 4, 2),
    (RELAY_CORE, 1, 2), (STEP, 4, 3), (STEP, 4, 4), (STEP, 4, 5), (STEP, 5, 0), (STEP, 5, 1),
    (CROSS, 3, 2), (CROSS, 3, 0), (CROSS, 3, 1), (STEP, 5, 2), (STEP, 5, 3), (STEP, 5, 4),
    (STEP, 5, 5), (REDUCE_NEAR, 3, 2), (STEP, 6, 0), (STEP, 6, 1), (CROSS, 2, 3), (CROSS, 2, 0),
    (CROSS, 2, 2), (REDUCE_NEAR, 3, 0), (STEP, 6, 2), (REDUCE_NEAR, 3, 1), (STEP, 6, 3),
    (STEP, 6, 4), (STEP, 6, 5), (REDUCE_NEAR, 2, 3), (CROSS, 3, 3), (CROSS, 2, 1), (PASS_CORE, 4),
    (REDUCE_NEAR, 2, 0), (CROSS, 1, 1), (CROSS, 1, 3), (CROSS, 1, 2), (STEP, 7, 0), (STEP, 7, 1),
    (STEP, 7, 2), (REDUCE_NEAR, 3, 3), (STEP, 7, 3), (STEP, 7, 4), (REDUCE_NEAR, 2, 1),
    (STEP, 7, 5), (REDUCE_NEAR, 2, 2), (CROSS, 1, 0), (REDUCE_NEAR, 1, 1), (FINISH_SIDE, 0, 7),
    (FINISH_SIDE, 0, 6), (FINISH_SIDE, 0, 4), (REDUCE_NEAR, 1, 3), (FINISH_SIDE, 0, 5),
    (REDUCE_NEAR, 1, 2), (REDUCE_NEAR, 1, 0), (FINISH_OWN, 0, 0), (FINISH_OWN, 0, 7),
    (FINISH_OWN, 0, 1), (FINISH_OWN, 0, 6), (FINISH_OWN, 0, 2), (FINISH_OWN, 0, 4),
    (FINISH_OWN, 0, 3), (FINISH_OWN, 0, 5),
)
INNER = (
    (SEND_Y, 1), (SEND_Z, 7, AHEAD), (SEND_Z, 5, BEHIND), (SEND_Y, 3), (CROSS_FIRST,),
    (SEND_Z, 6, BEHIND), (SEND_Z, 4, AHEAD), (SEND_Y, 2), (SEND_Z, 6, AHEAD), (SEND_Z, 4, BEHIND),
    (SEND_CORE,), (PASS_CORE, 1), (SEND_Z, 5, AHEAD), (RELAY_OWN, 2, 7), (RELAY_OWN, 0, 6),
    (PASS_CORE, 3), (RELAY_OWN, 2, 4), (SEND_Y, 5), (PASS_CORE, 7), (PASS_Z, 7),
    (RELAY_OWN, 0, 7), (SEND_Z, 0, AHEAD), (RELAY_OWN, 0, 4), (PASS_CORE, 2), (RELAY_OWN, 2, 5),
    (RELAY_OWN, 0, 5), (RELAY_CORE, 0, 6), (RELAY_OWN, 0, 2), (SEND_Y, 0), (RELAY_OWN, 2, 6),
    (RELAY_CORE, 2, 4), (SEND_Z, 3, AHEAD), (RELAY_OWN, 0, 1), (RELAY_SIDE, 2, 7), (PASS_CORE, 5),
    (RELAY_OWN, 3, 7), (RELAY_SIDE, 0, 7), (RELAY_CORE, 0, 4), (RELAY_OWN, 2, 0),
    (SEND_Z, 0, BEHIND), (RELAY_OWN, 0, 3), (RELAY_CORE, 2, 5), (SEND_Y, 4), (RELAY_OWN, 0, 0),
    (RELAY_OWN, 3, 4), (RELAY_OWN, 3, 6), (RELAY_CORE, 0, 5), (SEND_Z, 1, AHEAD), (STEP, 0, 0),
    (RELAY_OWN, 3, 5), (RELAY_CORE, 0, 2), (SEND_Z, 7, BEHIND), (STEP, 0, 1), (PASS_CORE, 0),
    (RELAY_OWN, 2, 3), (STEP, 0, 2), (RELAY_OWN, 3, 1), (SEND_Y, 6), (STEP, 0, 3), (STEP, 0, 4),
    (STEP, 0, 5), (RELAY_CORE, 0, 1), (RELAY_SIDE, 3, 7), (STEP, 1, 0), (RELAY_OWN, 3, 3),
    (RELAY_CORE, 2, 0), (STEP, 1, 1), (RELAY_CORE, 0, 3), (STEP, 1, 2), (STEP, 1, 3),
    (RELAY_OWN, 2, 1), (SEND_Z, 1, BEHIND), (STEP, 1, 4), (STEP, 1, 5), (RELAY_CORE, 2, 6),
    (PASS_CORE, 4), (SEND_Z, 2, AHEAD), (SEND_Z, 2, BEHIND), (RELAY_CORE, 0, 0),
    (RELAY_OWN, 3, 2), (RELAY_OWN, 3, 0), (SEND_Z, 3, BEHIND), (RELAY_CORE, 3, 4), (CROSS, 1, 3),
    (CROSS, 1, 2), (CROSS, 1, 0), (STEP, 2, 0), (RELAY_CORE, 3, 6), (STEP, 2, 1),
    (RELAY_OWN, 2, 2), (STEP, 2, 2), (RELAY_CORE, 3, 5), (STEP, 2, 3), (RELAY_CORE, 2, 3),
    (STEP, 2, 4), (STEP, 2, 5), (RELAY_CORE, 3, 1), (STEP, 3, 0), (STEP, 3, 1),
    (REDUCE_SIDE, 2, 6), (PASS_CORE, 6), (REDUCE_FAR, 2, 5), (REDUCE_FAR, 2, 6),
    (REDUCE_FAR, 2, 4), (REDUCE_SIDE, 2, 5), (REDUCE_SIDE, 2, 4), (STEP, 3, 2),
    (RELAY_CORE, 3, 3), (STEP, 3, 3), (STEP, 3, 4), (RELAY_CORE, 2, 1), (STEP, 3, 5),
    (STEP, 4, 0), (STEP, 4, 1), (RELAY_CORE, 3, 0), (CROSS, 0, 0), (STEP, 4, 2), (STEP, 4, 3),
    (STEP, 4, 4), (STEP, 4, 5), (STEP, 5, 0), (STEP, 5, 1), (FINISH_SIDE, 1, 6), (STEP, 5, 2),
    (STEP, 5, 3), (STEP, 5, 4), (STEP, 5, 5), (RELAY_CORE, 2, 2), (REDUCE_FAR, 2, 7),
    (FINISH_OWN, 1, 6), (CROSS, 0, 3), (RELAY_CORE, 3, 2), (CROSS, 0, 1), (CROSS, 1, 1),
    (REDUCE_SIDE, 2, 7), (CROSS, 0, 2), (REDUCE_FAR, 3, 5), (REDUCE_FAR, 3, 6),
    (REDUCE_FAR, 3, 4), (REDUCE_SIDE, 3, 4), (REDUCE_SIDE, 3, 6), (REDUCE_SIDE, 3, 7),
    (STEP, 6, 0), (FINISH_SIDE, 1, 5), (STEP, 6, 1), (STEP, 6, 2), (STEP, 6, 3),
    (FINISH_SIDE, 1, 7), (STEP, 6, 4), (REDUCE_FAR, 0, 5), (STEP, 6, 5), (STEP, 7, 0),
    (REDUCE_FAR, 0, 6), (REDUCE_SIDE, 3, 5), (STEP, 7, 1), (CROSS, 3, 0), (REDUCE_FAR, 0, 4),
    (CROSS, 3, 1), (REDUCE_FAR, 3, 7), (CROSS, 3, 3), (CROSS, 3, 2), (STEP, 7, 2), (STEP, 7, 3),
    (STEP, 7, 4), (REDUCE_SIDE, 0, 6), (STEP, 7, 5), (REDUCE_NEAR, 3, 0), (REDUCE_SIDE, 0, 4),
    (FINISH_OWN, 1, 7), (FINISH_OWN, 1, 5), (FINISH_SIDE, 1, 4), (REDUCE_SIDE, 0, 7),
    (REDUCE_NEAR, 3, 1), (CROSS, 2, 1), (CROSS, 2, 0), (CROSS, 2, 3), (CROSS, 2, 2),
    (REDUCE_SIDE, 0, 5), (REDUCE_FAR, 0, 7), (REDUCE_NEAR, 3, 2), (REDUCE_NEAR, 0, 0),
    (REDUCE_NEAR, 3, 3), (FINISH_OWN, 1, 4), (REDUCE_NEAR, 0, 1), (REDUCE_NEAR, 2, 1),
    (REDUCE_NEAR, 0, 2), (REDUCE_NEAR, 2, 0), (REDUCE_NEAR, 0, 3), (REDUCE_NEAR, 2, 3),
    (FINISH_OWN, 1, 1), (REDUCE_NEAR, 2, 2), (FINISH_OWN, 1, 3), (FINISH_OWN, 1, 0),
    (FINISH_OWN, 1, 2),
)
ROOM = 56 * 2**20


def tile_of(extent, most):
    return most if extent % most == 0 else extent


def needs(q, nz, task):
    name, *at = task
    if name in (CROSS_FIRST, SEND_Z, SEND_Y, SEND_CORE):
        return []
    if name in (PASS_Z, PASS_CORE):
        return [(FROM_Y, q, at[0])]
    p, k = at
    if name == RELAY_OWN:
        return [(OWN, p, k)]
    if name == RELAY_SIDE:
        return [(SIDE, p, k)]
    if name == RELAY_CORE:
        return [(FROM_Y, p, k)]
    h = 0 if k >= CHUNKS // 2 else 1
    own, side = ([(share, p, h, t) for t in range(2)] for share in (SHARE_OWN, SHARE_SIDE))
    if p == q:
        came = [w for w, there in ((AHEAD, q > 0), (BEHIND, q < nz - 1)) if there]
    else:
        came = [w for w, there in ((AHEAD, p > q > 0), (BEHIND, p < q < nz - 1)) if there]
    far = [(SUM_Z, p, CHUNKS + k - NEAR_OUT, w) for w in came]
    mine = [(SUM_Z, p, k, w) for w in came]
    cross = [(SUM_Y, p, k)]
    return {
        CROSS: side, REDUCE_SIDE: side + far, FINISH_SIDE: side + far,
        REDUCE_FAR: own + mine, REDUCE_NEAR: own + cross + mine, FINISH_OWN: own + cross + mine,
    }[name]


def hooks(q, nz, tasks):
    at, waited = (-1, STEPS - 1), set()
    plan = {at: []}

    def fresh(keys):
        news = [key for key in keys if key not in waited]
        waited.update(news)
        return news

    for task in tasks:
        if task[0] != STEP:
            plan[at].append((fresh(needs(q, nz, task)), task))
            continue
        if task[2] == 0:
            p, h = UNITS[q][task[1]]
            half = range(CHUNKS // 2, CHUNKS) if h == 0 else range(CHUNKS // 2)
            keys = [(core, p, k) for core in (CORE_OWN, CORE_SIDE) for k in half]
            keys += [(FROM_Y, p, k) for k in half if p == q or k < NEAR_IN]
            if p != q:
                keys += [(OWN, p, k) for k in half]
                keys += [(SIDE, p, k) for k in half if k >= NEAR_IN]
            plan[at].append((fresh(keys), None))
        at = (task[1], task[2])
        plan[at] = []
    return plan


def fused(
    n, hot, part, tok, routes, pick, gts, wg_in, wu_in, wd_in, hg_in, hu_in, hd_in, out,
    xs, keep, sc, rc, sy, ry, sz, rz, wg, wu, wd, wh, hid, hhid, cs, ct, gw,
    wsem, tsem, cts, ctr, up_s, down_s, z_r, y_s, y_r, c_s, c_r,
    rc_s, rc_r, ry_s, ry_r, rz_s, rz_r,
):
    nz = n // 4
    rows, model = tok.shape
    units = wg.shape[1]
    pad = hhid.shape[1]
    piece = rows // CHUNKS
    half = rows // 2
    wide = units // 3
    band = model // 2
    tile = tile_of(band, 512)
    me = lax.axis_index("expert")
    c = lax.rem(me, 2)
    y = lax.rem(lax.div(me, 2), 2)
    z = lax.div(me, 4)
    own = y * 2 + c
    side = (1 - y) * 2 + c
    peer_y = z * 4 + side
    peer_c = z * 4 + y * 2 + (1 - c)
    outer = (z == 0) | (z == nz - 1)
    low = z * 2 < nz

    def plane(p):
        return jnp.where(low, p, nz - 1 - p)

    ahead = me + jnp.where(low, 4, -4)
    behind = me - jnp.where(low, 4, -4)

    def remote(src, dst, send, recv, device):
        return pltpu.make_async_remote_copy(
            src_ref=src, dst_ref=dst, send_sem=send, recv_sem=recv,
            device_id={"expert": device}, device_id_type=pl.DeviceIdType.MESH,
        )

    def span(k):
        return pl.ds(k * piece, piece)

    loads = [
        pltpu.make_async_copy(src, dst, wsem.at[i])
        for i, (src, dst) in enumerate((
            *(
                (src.at[h], wh.at[pl.ds(t * pad + h * part, part)])
                for t, src in enumerate((hg_in, hu_in, hd_in)) for h in range(hot)
            ),
            (wg_in, wg), (wu_in, wu), (wd_in, wd),
        ))
    ]
    first = pltpu.make_async_copy(tok, xs.at[z, own], tsem)
    first.start()
    barrier = pltpu.get_barrier_semaphore()

    @pl.loop(1, n)
    def _(i):
        pl.semaphore_signal(
            barrier, inc=1, device_id={"expert": lax.rem(me + i, n)},
            device_id_type=pl.DeviceIdType.MESH,
        )

    ct[...] = jnp.zeros_like(ct)
    micros = gts.shape[0]

    def joined(parts):
        return jnp.concatenate(parts, axis=1)

    warm_row = joined([gts[m, 0:1, :] for m in range(micros)])
    chosen = joined([pick[m : m + 1, :] for m in range(micros)])
    named = [
        (
            joined([routes[k, m : m + 1, :] for m in range(micros)]),
            joined([gts[m, k + 1 : k + 2, :] for m in range(micros)]),
        )
        for k in range(routes.shape[0])
    ]

    def row(e):
        return sum(jnp.where(route == e, weight, 0.0) for route, weight in named)

    for e in range(n):
        ct[e, 0:1, :] = row(e)
        for h in range(hot):
            ct[e, 1 + h : 2 + h, :] = jnp.where(chosen == h, warm_row, 0.0)

    cs[me] = ct[me]
    first.wait()
    for load in loads:
        load.start()
    pl.semaphore_wait(barrier, n - 1)

    def ct_copy(i):
        peer = lax.rem(me + i, n)
        return remote(ct.at[peer], cs.at[me], cts.at[i], ctr.at[me], peer)

    def go_z(way, p, slot, k):
        at = k if slot is own else CHUNKS + k - NEAR_IN
        ref = xs.at[plane(p), slot, span(k)]
        send = up_s if way == AHEAD else down_s
        return remote(
            ref, ref, send.at[plane(p), at], z_r.at[plane(p), at],
            ahead if way == AHEAD else behind,
        )

    def go_y(p, k):
        ref = xs.at[plane(p), own, span(k)]
        return remote(ref, ref, y_s.at[plane(p), k], y_r.at[plane(p), k], peer_y)

    def go_c(p, which, k):
        ref = xs.at[plane(p), (own, side)[which], span(k)]
        return remote(
            ref, ref, c_s.at[plane(p), which, k], c_r.at[plane(p), which, k], peer_c
        )

    def share(at, h, j, t):
        lines = pl.ds(pl.multiple_of((1 - h) * half, half), half)
        cols = pl.ds(t * band, band)
        return remote(
            sc.at[at, j, lines, cols], rc.at[at, j, lines, cols],
            rc_s.at[at, h, j, t], rc_r.at[at, h, j, t], peer_c,
        )

    def share_y(p, k):
        at = plane(p)
        return remote(
            sy.at[at, span(k)], ry.at[at, span(k)], ry_s.at[at, k], ry_r.at[at, k], peer_y
        )

    def landing(way, p, last):
        if not last:
            return plane(p)
        return jnp.where(low == (way == AHEAD), plane(p), nz)

    def share_z(way, q, p, at):
        slot = landing(way, p, p == (q + 1 if way == AHEAD else q - 1))
        return remote(
            sz.at[plane(p), span(at)], rz.at[slot, span(at)],
            rz_s.at[plane(p), at], rz_r.at[slot, at],
            ahead if way == AHEAD else behind,
        )

    def await_event(q, key):
        name, p, k, *rest = key
        if name == OWN:
            go_z(AHEAD, p, own, k).wait_recv()
        elif name == SIDE:
            go_z(AHEAD, p, side, k).wait_recv()
        elif name == FROM_Y:
            ref = xs.at[plane(p), side, span(k)]
            remote(ref, ref, y_s.at[plane(p), k], y_r.at[plane(p), k], peer_y).wait_recv()
        elif name in (CORE_OWN, CORE_SIDE):
            go_c(p, int(name == CORE_SIDE), k).wait_recv()
        elif name in (SHARE_OWN, SHARE_SIDE):
            share(plane(p), k, y if name == SHARE_OWN else 1 - y, rest[0]).wait_recv()
        elif name == SUM_Y:
            share_y(p, k).wait_recv()
        else:
            slot = landing(rest[0], p, p == q)
            ref = rz.at[slot, span(k)]
            remote(ref, ref, rz_s.at[0, k], rz_r.at[slot, k], me).wait_recv()

    def ways(q, p):
        return (AHEAD,) * (p <= q and q + 1 < nz) + (BEHIND,) * (p >= q and q > 0)

    def add_up(dst, lines, terms):
        @pl.loop(0, model // tile)
        def _(t):
            cols = pl.ds(pl.multiple_of(t * tile, tile), tile)
            total = None
            for term in terms:
                value = term(cols).astype(jnp.float32)
                total = value if total is None else total + value
            dst[lines, cols] = total.astype(jnp.bfloat16)

    def act(q, task):
        name, *at = task
        if name == CROSS_FIRST:
            for k in HIGH + LOW:
                if k >= NEAR_IN:
                    go_y(q, k).start()
        elif name == SEND_Z:
            go_z(at[1], q, own, at[0]).start()
        elif name == SEND_CORE:
            for k in range(CHUNKS):
                go_c(q, 0, k).start()
        elif name == PASS_Z:
            for way in ways(q, q):
                go_z(way, q, side, at[0]).start()
        elif name == SEND_Y:
            go_y(q, at[0]).start()
        elif name == PASS_CORE:
            go_c(q, 1, at[0]).start()
        elif name == RELAY_OWN:
            p, k = at
            for way in ways(q, p):
                go_z(way, p, own, k).start()
            if k < NEAR_IN:
                go_y(p, k).start()
            go_c(p, 0, k).start()
        elif name == RELAY_SIDE:
            p, k = at
            for way in ways(q, p):
                go_z(way, p, side, k).start()
            go_c(p, 1, k).start()
        elif name == RELAY_CORE:
            go_c(at[0], 1, at[1]).start()
        else:
            p, k = at
            j = 1 - y if name in (CROSS, REDUCE_SIDE, FINISH_SIDE) else y
            here = plane(p)
            terms = [
                lambda cols: keep[here, j, span(k), cols],
                lambda cols: rc[here, j, span(k), cols],
            ]
            for key in needs(q, nz, task):
                if key[0] == SUM_Y:
                    terms.append(lambda cols: ry[here, span(k), cols])
                if key[0] == SUM_Z:
                    slot, line = landing(key[3], p, p == q), span(key[2])
                    terms.append(lambda cols, slot=slot, line=line: rz[slot, line, cols])
            if name in (CROSS, FINISH_SIDE):
                add_up(sy.at[here], span(k), terms)
                share_y(p, k).start()
            elif name == FINISH_OWN:
                add_up(out, span(k), terms)
            else:
                line = CHUNKS + k - NEAR_OUT if name == REDUCE_SIDE else k
                add_up(sz.at[here], span(line), terms)
                share_z(AHEAD if p > q else BEHIND, q, p, line).start()

    plans = [hooks(q, nz, tasks) for q, tasks in enumerate((OUTER, INNER))]

    def perform(q, steps):
        for keys, task in steps:
            for key in keys:
                await_event(q, key)
            if task is not None:
                act(q, task)

    def by_class(emit):
        @pl.when(outer)
        def _():
            emit(0)

        @pl.when(jnp.logical_not(outer))
        def _():
            emit(1)

    count = len(UNITS[0])

    def hook(u, step):
        def emit(q):
            for j in range(count):
                if (j, step) != (count - 1, STEPS - 1) and plans[q].get((j, step)):
                    @pl.when(u == j)
                    def _():
                        perform(q, plans[q][j, step])

        by_class(emit)

    def picked(u, field):
        found = [
            functools.reduce(
                lambda rest, j: jnp.where(u == j, UNITS[q][j][field], rest),
                range(1, count), jnp.int32(UNITS[q][0][field]),
            )
            for q in range(2)
        ]
        return jnp.where(outer, *found)

    def take_tables():
        if pad > hot * part:
            for t in range(3):
                blank = wh.at[pl.ds(t * pad + hot * part, pad - hot * part)]
                blank[...] = jnp.zeros_like(blank)

        for load in loads:
            load.wait()

        @pl.loop(1, n)
        def _(i):
            other = lax.rem(me + i, n)
            remote(
                ct.at[other], cs.at[other], cts.at[i], ctr.at[other], other
            ).wait_recv()

        @pl.loop(0, n)
        def _(e):
            gw[e] = jnp.transpose(cs[e])

    def start(q):
        for keys, task in plans[q][-1, STEPS - 1]:
            if task is None:
                take_tables()
            perform(q, [(keys, task)])

    @pl.loop(1, n)
    def _(i):
        ct_copy(i).start()

    by_class(start)

    @pl.loop(0, count)
    def _(u):
        here = plane(picked(u, 0))
        h = picked(u, 1)
        lines = pl.ds(pl.multiple_of((1 - h) * half, half), half)

        def block():
            return xs[here, :, lines, :].reshape(4 * half, model)

        def columns(which):
            return jnp.concatenate(
                [gw[here * 4 + j, lines, which : which + 1] for j in range(4)], axis=0
            )

        for i in range(3):
            cols = pl.ds(i * wide, wide)
            v = block()
            g = jnp.dot(v, wg[:, cols], preferred_element_type=jnp.float32)
            up = jnp.dot(v, wu[:, cols], preferred_element_type=jnp.float32)
            hid[:, cols] = (g / (1.0 + jnp.exp(-g)) * up).astype(jnp.bfloat16)
            hook(u, i)

        gu = lax.dot_general(
            block(), wh[: 2 * pad, :], (((1,), (1,)), ((), ())),
            preferred_element_type=jnp.float32,
        )
        g, up = gu[:, :pad], gu[:, pad:]
        lane = lax.broadcasted_iota(jnp.int32, (4 * half, pad), 1)
        warm = jnp.zeros((4 * half, pad), jnp.float32)
        for i in range(hot):
            warm = jnp.where((lane >= i * part) & (lane < (i + 1) * part), columns(1 + i), warm)
        hhid[...] = (g / (1.0 + jnp.exp(-g)) * up * warm).astype(jnp.bfloat16)
        hook(u, 3)

        cold = columns(0)
        for t in range(2):
            for i in range(band // tile):
                cols = pl.ds(t * band + i * tile, tile)
                r = jnp.dot(hid[...], wd[:, cols], preferred_element_type=jnp.float32)
                r = r.astype(jnp.bfloat16).astype(jnp.float32) * cold
                r = r + jnp.dot(
                    hhid[...], wh[2 * pad :, cols], preferred_element_type=jnp.float32
                )
                for j in range(2):
                    even = r[2 * j * half : (2 * j + 1) * half]
                    odd = r[(2 * j + 1) * half : (2 * j + 2) * half]
                    keep[here, j, lines, cols] = jnp.where(c == 0, even, odd)
                    sc[here, j, lines, cols] = jnp.where(c == 0, odd, even).astype(jnp.bfloat16)
            share(here, h, 1 - y, t).start()
            share(here, h, y, t).start()
            hook(u, 4 + t)

    by_class(lambda q: perform(q, plans[q][count - 1, STEPS - 1]))

    @pl.loop(1, n)
    def _(i):
        ct_copy(i).wait_send()

    def settle(q):
        for p in range(nz):
            for k in range(CHUNKS):
                for way in ways(q, p):
                    go_z(way, p, own, k).wait_send()
                    if k >= NEAR_IN:
                        go_z(way, p, side, k).wait_send()
                if k < NEAR_IN or p == q:
                    go_y(p, k).wait_send()
                go_c(p, 0, k).wait_send()
                go_c(p, 1, k).wait_send()
                if k < NEAR_OUT or p == q:
                    share_y(p, k).wait_send()
            for h in range(2):
                for j in range(2):
                    for t in range(2):
                        share(plane(p), h, j, t).wait_send()
            if p != q:
                for at in range(2 * CHUNKS - NEAR_OUT):
                    share_z(AHEAD if p > q else BEHIND, q, p, at).wait_send()

    by_class(settle)


def scratch(n, rows, model, units, pad, hot):
    nz = n // 4
    half, full = jnp.bfloat16, jnp.float32
    dma = pltpu.SemaphoreType.DMA
    piece = rows // CHUNKS
    gathers, reduces = 2 * CHUNKS - NEAR_IN, 2 * CHUNKS - NEAR_OUT
    return [
        pltpu.VMEM((nz, 4, rows, model), half),
        pltpu.VMEM((nz, 2, rows, model), full),
        pltpu.VMEM((nz, 2, rows, model), half),
        pltpu.VMEM((nz, 2, rows, model), half),
        pltpu.VMEM((nz, rows, model), half),
        pltpu.VMEM((nz, rows, model), half),
        pltpu.VMEM((nz, reduces * piece, model), half),
        pltpu.VMEM((nz + 1, reduces * piece, model), half),
        pltpu.VMEM((model, units), half),
        pltpu.VMEM((model, units), half),
        pltpu.VMEM((units, model), half),
        pltpu.VMEM((3 * pad, model), half),
        pltpu.VMEM((2 * rows, units), half),
        pltpu.VMEM((2 * rows, pad), half),
        pltpu.VMEM((n, 8, rows), full),
        pltpu.VMEM((n, 8, rows), full),
        pltpu.VMEM((n, rows, 8), full),
        dma((3 + 3 * hot,)), dma, dma((n,)), dma((n,)),
        dma((nz, gathers)), dma((nz, gathers)), dma((nz, gathers)),
        dma((nz, CHUNKS)), dma((nz, CHUNKS)), dma((nz, 2, CHUNKS)), dma((nz, 2, CHUNKS)),
        dma((nz, 2, 2, 2)), dma((nz, 2, 2, 2)),
        dma((nz, CHUNKS)), dma((nz, CHUNKS)),
        dma((nz, reduces)), dma((nz + 1, reduces)),
    ]


def shards(tokens, w_gate, w_up, w_down, hot_gate, hot_up, hot_down, cold_routes, hot_pick, gates):
    n = lax.axis_size("expert")
    micro_count, local_tokens, model = tokens.shape
    rows = micro_count * local_tokens
    hot, units, part = hot_gate.shape[0], w_gate.shape[2], hot_gate.shape[2]
    pad = -(-hot * part // 128) * 128
    need = rows * model * n * 9 + 3 * model * (units + pad) * 2
    if n != 16 or part % 16 or rows % (16 * CHUNKS) or units % 384 or model % 256 or need > ROOM or hot > 7:
        return routed(
            tokens, w_gate, w_up, w_down, hot_gate, hot_up, hot_down, cold_routes, hot_pick, gates
        )
    anyplace = pl.BlockSpec(memory_space=pl.ANY)
    vmem = pl.BlockSpec(memory_space=pltpu.VMEM)
    mixed = pl.pallas_call(
        functools.partial(fused, n, hot, part),
        out_shape=jax.ShapeDtypeStruct((rows, model), jnp.bfloat16),
        in_specs=[anyplace, vmem, vmem, vmem] + [anyplace] * 6,
        out_specs=vmem,
        scratch_shapes=scratch(n, rows, model, units, pad, hot),
        compiler_params=pltpu.CompilerParams(
            collective_id=0, has_side_effects=True, vmem_limit_bytes=64 * 2**20 - 2**17
        ),
    )(
        tokens.reshape(rows, model), jnp.transpose(cold_routes, (2, 0, 1)), hot_pick,
        jnp.swapaxes(gates, 1, 2),
        w_gate[0], w_up[0], w_down[0],
        *(jnp.swapaxes(w, 1, 2) for w in (hot_gate, hot_up, hot_down)),
    )
    return mixed.reshape(tokens.shape)


def solution(mesh):
    in_specs = (
        P(None, ("groups", "expert"), None),
        P("expert", None, None),
        P("expert", None, None),
        P("expert", None, None),
        P(None, None, "expert"),
        P(None, None, "expert"),
        P(None, None, "expert"),
        P(None, ("groups", "expert"), None),
        P(None, ("groups", "expert")),
        P(None, ("groups", "expert"), None),
    )
    out_specs = P(None, ("groups", "expert"), None)
    return jax.shard_map(shards, mesh=mesh, in_specs=in_specs, out_specs=out_specs, check_vma=False)
```

time: 130 us -> 95.1 us (0.73)
  Pallas kernels: 128 us -> 92.9 us
    pallas_call x1, Pallas kernels: 128 us -> 92.9 us  [shards(): pl.pallas_call(functools.partial(fused, n, hot, part), out_shape=jax.Shap...]
where the time goes in v2:
time: 95.1 us; the launch traced here: 94.8 us
  Pallas kernels  92.9 us (98%)
  local copies, waits for them, and re-layouts  1.88 us (2%)
    pallas_call x1, Pallas kernels, shards(): pl.pallas_call(functools.partial(fused, n, hot, part), out_shape=jax.Shap...  92.9 us

profile of v2, /device:TPU:0, one launch (start us, length us, event | category | flops | bytes accessed | tf_op | source)
XLA Modules:
  0.0 94.8 jit_solution(17662820734815946680)
XLA Ops:
  0.0 92.9 %shard_map.100 = bf16[128,2048]{1,0:T(8,128)(2,1)} custom-call(bf16[128,2048]{1,0:T(8,128)(2,1)} %bitcast.14, s32[7,2,64]{2,1,0:T(2,128)} %bitcast.19, s32[2,64]{1,0:T(2,128)} %pick.1, f32[2,8,64]{2,1,0:T(8,128)} %bitcast.18, bf16[2048,768]{1,0:T(8,128)(2,1)} %bitcast.10, bf16[2048,768]{1,0:T(8,128)(2,1)} %bitcast.11, bf16[768,2048]{1,0:T(8,128)(2,1)} %bitcast.12, ...), custom_call_target="tpu_custom_call" | custom-call | tf_op jit(solution)/shard_map/pallas_call | solution.py:696
  93.0 1.9 %copy.12 = bf16[2,64,2048]{2,1,0:T(8,128)(2,1)} copy(bf16[2,64,2048]{2,1,0:T(8,128)(2,1)} %bitcast.13) | data formatting | bytes 1048576

commit v3 on v2

--- a/solution.py
+++ b/solution.py
@@ -109,96 +109,97 @@
 AHEAD, BEHIND = range(2)
 CHUNKS = 8
 NEAR_IN = 7
-NEAR_OUT = 4
-HIGH = (5, 4, 6, 7)
-LOW = (3, 2, 0, 1)
+NEAR_OUT = 5
+HIGH = (4, 6, 7, 5)
+LOW = (2, 1, 3, 0)
 STEPS = 6
+TABLE_WITH = 4
 UNITS = (
-    ((2, 0), (1, 0), (3, 0), (0, 1), (3, 1), (2, 1), (1, 1), (0, 0)),
-    ((0, 0), (1, 1), (2, 0), (0, 1), (1, 0), (3, 0), (3, 1), (2, 1)),
+    ((1, 0), (0, 0), (2, 0), (3, 0), (1, 1), (3, 1), (2, 1), (0, 1)),
+    ((1, 1), (0, 0), (3, 0), (2, 0), (3, 1), (0, 1), (2, 1), (1, 0)),
 )
 OUTER = (
-    (SEND_Z, 6, AHEAD), (SEND_CORE,), (SEND_Y, 6), (CROSS_FIRST,), (SEND_Z, 7, AHEAD),
-    (SEND_Z, 4, AHEAD), (SEND_Y, 2), (RELAY_OWN, 1, 5), (SEND_Y, 1), (SEND_Z, 5, AHEAD),
-    (PASS_CORE, 6), (SEND_Z, 2, AHEAD), (SEND_Z, 1, AHEAD), (PASS_Z, 7), (SEND_Z, 3, AHEAD),
-    (PASS_CORE, 7), (RELAY_OWN, 1, 4), (PASS_CORE, 2), (RELAY_OWN, 2, 7), (RELAY_CORE, 1, 5),
-    (RELAY_OWN, 2, 4), (PASS_CORE, 1), (RELAY_SIDE, 1, 7), (RELAY_CORE, 1, 4), (RELAY_OWN, 2, 5),
-    (SEND_Z, 0, AHEAD), (RELAY_CORE, 2, 4), (RELAY_OWN, 2, 6), (SEND_Y, 0), (RELAY_SIDE, 2, 7),
-    (RELAY_CORE, 2, 5), (RELAY_OWN, 3, 7), (RELAY_CORE, 2, 6), (STEP, 0, 0), (RELAY_OWN, 2, 0),
-    (PASS_CORE, 0), (RELAY_OWN, 1, 6), (STEP, 0, 1), (STEP, 0, 2), (RELAY_OWN, 3, 4),
-    (STEP, 0, 3), (STEP, 0, 4), (RELAY_OWN, 3, 6), (STEP, 0, 5), (RELAY_CORE, 2, 0),
-    (RELAY_CORE, 1, 6), (SEND_Y, 5), (RELAY_OWN, 3, 5), (RELAY_OWN, 1, 0), (REDUCE_FAR, 2, 4),
-    (REDUCE_FAR, 2, 6), (REDUCE_FAR, 2, 5), (REDUCE_FAR, 2, 7), (REDUCE_SIDE, 2, 7),
-    (REDUCE_SIDE, 2, 5), (REDUCE_SIDE, 2, 4), (RELAY_CORE, 3, 4), (REDUCE_SIDE, 2, 6),
-    (RELAY_OWN, 1, 7), (RELAY_CORE, 3, 6), (STEP, 1, 0), (RELAY_OWN, 2, 3), (STEP, 1, 1),
-    (PASS_CORE, 5), (RELAY_OWN, 3, 1), (STEP, 1, 2), (RELAY_CORE, 3, 5), (RELAY_SIDE, 3, 7),
-    (STEP, 1, 3), (STEP, 1, 4), (RELAY_CORE, 1, 0), (SEND_Y, 3), (RELAY_OWN, 3, 3), (STEP, 1, 5),
-    (STEP, 2, 0), (RELAY_CORE, 2, 3), (RELAY_OWN, 2, 1), (REDUCE_FAR, 1, 6), (STEP, 2, 1),
-    (RELAY_OWN, 1, 1), (RELAY_CORE, 3, 1), (REDUCE_SIDE, 1, 6), (STEP, 2, 2), (PASS_CORE, 3),
-    (STEP, 2, 3), (STEP, 2, 4), (RELAY_CORE, 3, 3), (STEP, 2, 5), (RELAY_OWN, 3, 2), (STEP, 3, 0),
-    (RELAY_OWN, 3, 0), (REDUCE_FAR, 3, 6), (REDUCE_FAR, 3, 5), (RELAY_CORE, 2, 1),
-    (REDUCE_FAR, 3, 4), (REDUCE_SIDE, 3, 7), (REDUCE_SIDE, 3, 6), (REDUCE_SIDE, 3, 4),
-    (STEP, 3, 1), (RELAY_OWN, 1, 3), (RELAY_CORE, 1, 1), (STEP, 3, 2), (RELAY_OWN, 2, 2),
-    (SEND_Y, 4), (STEP, 3, 3), (STEP, 3, 4), (RELAY_CORE, 3, 0), (STEP, 3, 5), (REDUCE_FAR, 1, 4),
-    (RELAY_OWN, 1, 2), (REDUCE_FAR, 1, 5), (RELAY_CORE, 1, 3), (REDUCE_SIDE, 1, 5),
-    (REDUCE_FAR, 1, 7), (REDUCE_SIDE, 1, 7), (REDUCE_SIDE, 1, 4), (REDUCE_SIDE, 3, 5),
-    (REDUCE_FAR, 3, 7), (RELAY_CORE, 3, 2), (CROSS, 0, 3), (CROSS, 0, 1), (CROSS, 0, 0),
-    (CROSS, 0, 2), (RELAY_CORE, 2, 2), (STEP, 4, 0), (STEP, 4, 1), (STEP, 4, 2),
-    (RELAY_CORE, 1, 2), (STEP, 4, 3), (STEP, 4, 4), (STEP, 4, 5), (STEP, 5, 0), (STEP, 5, 1),
-    (CROSS, 3, 2), (CROSS, 3, 0), (CROSS, 3, 1), (STEP, 5, 2), (STEP, 5, 3), (STEP, 5, 4),
-    (STEP, 5, 5), (REDUCE_NEAR, 3, 2), (STEP, 6, 0), (STEP, 6, 1), (CROSS, 2, 3), (CROSS, 2, 0),
-    (CROSS, 2, 2), (REDUCE_NEAR, 3, 0), (STEP, 6, 2), (REDUCE_NEAR, 3, 1), (STEP, 6, 3),
-    (STEP, 6, 4), (STEP, 6, 5), (REDUCE_NEAR, 2, 3), (CROSS, 3, 3), (CROSS, 2, 1), (PASS_CORE, 4),
-    (REDUCE_NEAR, 2, 0), (CROSS, 1, 1), (CROSS, 1, 3), (CROSS, 1, 2), (STEP, 7, 0), (STEP, 7, 1),
-    (STEP, 7, 2), (REDUCE_NEAR, 3, 3), (STEP, 7, 3), (STEP, 7, 4), (REDUCE_NEAR, 2, 1),
-    (STEP, 7, 5), (REDUCE_NEAR, 2, 2), (CROSS, 1, 0), (REDUCE_NEAR, 1, 1), (FINISH_SIDE, 0, 7),
-    (FINISH_SIDE, 0, 6), (FINISH_SIDE, 0, 4), (REDUCE_NEAR, 1, 3), (FINISH_SIDE, 0, 5),
-    (REDUCE_NEAR, 1, 2), (REDUCE_NEAR, 1, 0), (FINISH_OWN, 0, 0), (FINISH_OWN, 0, 7),
-    (FINISH_OWN, 0, 1), (FINISH_OWN, 0, 6), (FINISH_OWN, 0, 2), (FINISH_OWN, 0, 4),
-    (FINISH_OWN, 0, 3), (FINISH_OWN, 0, 5),
+    (SEND_Y, 1), (SEND_CORE,), (SEND_Z, 4, AHEAD), (CROSS_FIRST,), (SEND_Z, 7, AHEAD),
+    (SEND_Y, 2), (SEND_Z, 6, AHEAD), (SEND_Y, 3), (PASS_CORE, 1), (SEND_Z, 5, AHEAD),
+    (RELAY_OWN, 1, 6), (PASS_Z, 7), (PASS_CORE, 7), (RELAY_OWN, 1, 4), (PASS_CORE, 2),
+    (SEND_Z, 2, AHEAD), (RELAY_OWN, 1, 5), (SEND_Z, 3, AHEAD), (SEND_Y, 4), (PASS_CORE, 3),
+    (SEND_Y, 6), (RELAY_OWN, 2, 4), (RELAY_CORE, 1, 6), (RELAY_SIDE, 1, 7), (RELAY_CORE, 1, 4),
+    (SEND_Z, 1, AHEAD), (RELAY_OWN, 1, 7), (SEND_Z, 0, AHEAD), (RELAY_CORE, 1, 5),
+    (RELAY_OWN, 1, 1), (SEND_Y, 5), (STEP, 0, 0), (PASS_CORE, 4), (RELAY_OWN, 2, 6), (STEP, 0, 1),
+    (STEP, 0, 2), (STEP, 0, 3), (STEP, 0, 4), (RELAY_OWN, 3, 4), (STEP, 0, 5), (PASS_CORE, 6),
+    (RELAY_OWN, 2, 5), (RELAY_CORE, 1, 1), (RELAY_OWN, 1, 3), (RELAY_CORE, 2, 4),
+    (REDUCE_FAR, 1, 7), (REDUCE_FAR, 1, 5), (REDUCE_FAR, 1, 6), (REDUCE_SIDE, 1, 5),
+    (REDUCE_SIDE, 1, 6), (REDUCE_SIDE, 1, 7), (PASS_CORE, 5), (CROSS, 1, 4), (RELAY_OWN, 2, 7),
+    (STEP, 1, 0), (RELAY_CORE, 2, 6), (RELAY_OWN, 1, 0), (STEP, 1, 1), (RELAY_OWN, 2, 0),
+    (RELAY_CORE, 3, 4), (STEP, 1, 2), (STEP, 1, 3), (RELAY_OWN, 1, 2), (RELAY_CORE, 2, 5),
+    (STEP, 1, 4), (STEP, 1, 5), (RELAY_SIDE, 2, 7), (RELAY_CORE, 1, 3), (REDUCE_NEAR, 1, 4),
+    (CROSS, 0, 4), (RELAY_OWN, 3, 6), (STEP, 2, 0), (STEP, 2, 1), (RELAY_OWN, 3, 5), (STEP, 2, 2),
+    (RELAY_SIDE, 3, 7), (STEP, 2, 3), (STEP, 2, 4), (STEP, 2, 5), (RELAY_CORE, 1, 2),
+    (RELAY_CORE, 2, 0), (RELAY_OWN, 3, 3), (RELAY_CORE, 1, 0), (SEND_Y, 0), (RELAY_OWN, 3, 0),
+    (REDUCE_FAR, 2, 7), (REDUCE_FAR, 2, 5), (REDUCE_FAR, 2, 6), (REDUCE_SIDE, 2, 5),
+    (REDUCE_SIDE, 2, 7), (REDUCE_SIDE, 2, 6), (CROSS, 2, 4), (RELAY_CORE, 3, 6),
+    (RELAY_OWN, 3, 7), (RELAY_CORE, 3, 5), (RELAY_OWN, 3, 1), (STEP, 3, 0), (RELAY_CORE, 3, 3),
+    (RELAY_OWN, 3, 2), (STEP, 3, 1), (RELAY_OWN, 2, 3), (PASS_CORE, 0), (STEP, 3, 2),
+    (STEP, 3, 3), (RELAY_CORE, 3, 0), (STEP, 3, 4), (STEP, 3, 5), (REDUCE_NEAR, 2, 4),
+    (RELAY_OWN, 2, 1), (RELAY_OWN, 2, 2), (STEP, 4, 0), (REDUCE_FAR, 3, 6), (REDUCE_FAR, 3, 7),
+    (STEP, 4, 1), (REDUCE_SIDE, 3, 7), (REDUCE_SIDE, 3, 6), (RELAY_CORE, 3, 1),
+    (REDUCE_SIDE, 3, 5), (CROSS, 3, 4), (STEP, 4, 2), (RELAY_CORE, 3, 2), (STEP, 4, 3),
+    (STEP, 4, 4), (RELAY_CORE, 2, 3), (STEP, 4, 5), (STEP, 5, 0), (STEP, 5, 1), (CROSS, 1, 3),
+    (CROSS, 1, 2), (CROSS, 1, 1), (STEP, 5, 2), (STEP, 5, 3), (REDUCE_NEAR, 3, 4), (STEP, 5, 4),
+    (STEP, 5, 5), (RELAY_CORE, 2, 2), (REDUCE_FAR, 3, 5), (REDUCE_NEAR, 1, 3), (CROSS, 1, 0),
+    (RELAY_CORE, 2, 1), (CROSS, 3, 3), (CROSS, 3, 0), (CROSS, 3, 2), (CROSS, 3, 1),
+    (REDUCE_NEAR, 1, 2), (STEP, 6, 0), (STEP, 6, 1), (REDUCE_NEAR, 1, 1), (STEP, 6, 2),
+    (REDUCE_NEAR, 1, 0), (STEP, 6, 3), (STEP, 6, 4), (STEP, 6, 5), (STEP, 7, 0),
+    (FINISH_SIDE, 0, 6), (REDUCE_NEAR, 3, 0), (STEP, 7, 1), (CROSS, 2, 3), (CROSS, 2, 2),
+    (STEP, 7, 2), (REDUCE_NEAR, 3, 2), (FINISH_OWN, 0, 4), (STEP, 7, 3), (STEP, 7, 4),
+    (REDUCE_NEAR, 3, 1), (STEP, 7, 5), (CROSS, 2, 0), (CROSS, 2, 1), (REDUCE_NEAR, 3, 3),
+    (FINISH_SIDE, 0, 7), (CROSS, 0, 0), (CROSS, 0, 3), (CROSS, 0, 2), (CROSS, 0, 1),
+    (REDUCE_NEAR, 2, 3), (REDUCE_NEAR, 2, 2), (REDUCE_NEAR, 2, 0), (FINISH_SIDE, 0, 5),
+    (REDUCE_NEAR, 2, 1), (FINISH_OWN, 0, 6), (FINISH_OWN, 0, 7), (FINISH_OWN, 0, 0),
+    (FINISH_OWN, 0, 2), (FINISH_OWN, 0, 3), (FINISH_OWN, 0, 1), (FINISH_OWN, 0, 5),
 )
 INNER = (
-    (SEND_Y, 1), (SEND_Z, 7, AHEAD), (SEND_Z, 5, BEHIND), (SEND_Y, 3), (CROSS_FIRST,),
-    (SEND_Z, 6, BEHIND), (SEND_Z, 4, AHEAD), (SEND_Y, 2), (SEND_Z, 6, AHEAD), (SEND_Z, 4, BEHIND),
-    (SEND_CORE,), (PASS_CORE, 1), (SEND_Z, 5, AHEAD), (RELAY_OWN, 2, 7), (RELAY_OWN, 0, 6),
-    (PASS_CORE, 3), (RELAY_OWN, 2, 4), (SEND_Y, 5), (PASS_CORE, 7), (PASS_Z, 7),
-    (RELAY_OWN, 0, 7), (SEND_Z, 0, AHEAD), (RELAY_OWN, 0, 4), (PASS_CORE, 2), (RELAY_OWN, 2, 5),
-    (RELAY_OWN, 0, 5), (RELAY_CORE, 0, 6), (RELAY_OWN, 0, 2), (SEND_Y, 0), (RELAY_OWN, 2, 6),
-    (RELAY_CORE, 2, 4), (SEND_Z, 3, AHEAD), (RELAY_OWN, 0, 1), (RELAY_SIDE, 2, 7), (PASS_CORE, 5),
-    (RELAY_OWN, 3, 7), (RELAY_SIDE, 0, 7), (RELAY_CORE, 0, 4), (RELAY_OWN, 2, 0),
-    (SEND_Z, 0, BEHIND), (RELAY_OWN, 0, 3), (RELAY_CORE, 2, 5), (SEND_Y, 4), (RELAY_OWN, 0, 0),
-    (RELAY_OWN, 3, 4), (RELAY_OWN, 3, 6), (RELAY_CORE, 0, 5), (SEND_Z, 1, AHEAD), (STEP, 0, 0),
-    (RELAY_OWN, 3, 5), (RELAY_CORE, 0, 2), (SEND_Z, 7, BEHIND), (STEP, 0, 1), (PASS_CORE, 0),
-    (RELAY_OWN, 2, 3), (STEP, 0, 2), (RELAY_OWN, 3, 1), (SEND_Y, 6), (STEP, 0, 3), (STEP, 0, 4),
-    (STEP, 0, 5), (RELAY_CORE, 0, 1), (RELAY_SIDE, 3, 7), (STEP, 1, 0), (RELAY_OWN, 3, 3),
-    (RELAY_CORE, 2, 0), (STEP, 1, 1), (RELAY_CORE, 0, 3), (STEP, 1, 2), (STEP, 1, 3),
-    (RELAY_OWN, 2, 1), (SEND_Z, 1, BEHIND), (STEP, 1, 4), (STEP, 1, 5), (RELAY_CORE, 2, 6),
-    (PASS_CORE, 4), (SEND_Z, 2, AHEAD), (SEND_Z, 2, BEHIND), (RELAY_CORE, 0, 0),
-    (RELAY_OWN, 3, 2), (RELAY_OWN, 3, 0), (SEND_Z, 3, BEHIND), (RELAY_CORE, 3, 4), (CROSS, 1, 3),
-    (CROSS, 1, 2), (CROSS, 1, 0), (STEP, 2, 0), (RELAY_CORE, 3, 6), (STEP, 2, 1),
-    (RELAY_OWN, 2, 2), (STEP, 2, 2), (RELAY_CORE, 3, 5), (STEP, 2, 3), (RELAY_CORE, 2, 3),
-    (STEP, 2, 4), (STEP, 2, 5), (RELAY_CORE, 3, 1), (STEP, 3, 0), (STEP, 3, 1),
-    (REDUCE_SIDE, 2, 6), (PASS_CORE, 6), (REDUCE_FAR, 2, 5), (REDUCE_FAR, 2, 6),
-    (REDUCE_FAR, 2, 4), (REDUCE_SIDE, 2, 5), (REDUCE_SIDE, 2, 4), (STEP, 3, 2),
-    (RELAY_CORE, 3, 3), (STEP, 3, 3), (STEP, 3, 4), (RELAY_CORE, 2, 1), (STEP, 3, 5),
-    (STEP, 4, 0), (STEP, 4, 1), (RELAY_CORE, 3, 0), (CROSS, 0, 0), (STEP, 4, 2), (STEP, 4, 3),
-    (STEP, 4, 4), (STEP, 4, 5), (STEP, 5, 0), (STEP, 5, 1), (FINISH_SIDE, 1, 6), (STEP, 5, 2),
-    (STEP, 5, 3), (STEP, 5, 4), (STEP, 5, 5), (RELAY_CORE, 2, 2), (REDUCE_FAR, 2, 7),
-    (FINISH_OWN, 1, 6), (CROSS, 0, 3), (RELAY_CORE, 3, 2), (CROSS, 0, 1), (CROSS, 1, 1),
-    (REDUCE_SIDE, 2, 7), (CROSS, 0, 2), (REDUCE_FAR, 3, 5), (REDUCE_FAR, 3, 6),
-    (REDUCE_FAR, 3, 4), (REDUCE_SIDE, 3, 4), (REDUCE_SIDE, 3, 6), (REDUCE_SIDE, 3, 7),
-    (STEP, 6, 0), (FINISH_SIDE, 1, 5), (STEP, 6, 1), (STEP, 6, 2), (STEP, 6, 3),
-    (FINISH_SIDE, 1, 7), (STEP, 6, 4), (REDUCE_FAR, 0, 5), (STEP, 6, 5), (STEP, 7, 0),
-    (REDUCE_FAR, 0, 6), (REDUCE_SIDE, 3, 5), (STEP, 7, 1), (CROSS, 3, 0), (REDUCE_FAR, 0, 4),
-    (CROSS, 3, 1), (REDUCE_FAR, 3, 7), (CROSS, 3, 3), (CROSS, 3, 2), (STEP, 7, 2), (STEP, 7, 3),
-    (STEP, 7, 4), (REDUCE_SIDE, 0, 6), (STEP, 7, 5), (REDUCE_NEAR, 3, 0), (REDUCE_SIDE, 0, 4),
-    (FINISH_OWN, 1, 7), (FINISH_OWN, 1, 5), (FINISH_SIDE, 1, 4), (REDUCE_SIDE, 0, 7),
-    (REDUCE_NEAR, 3, 1), (CROSS, 2, 1), (CROSS, 2, 0), (CROSS, 2, 3), (CROSS, 2, 2),
-    (REDUCE_SIDE, 0, 5), (REDUCE_FAR, 0, 7), (REDUCE_NEAR, 3, 2), (REDUCE_NEAR, 0, 0),
-    (REDUCE_NEAR, 3, 3), (FINISH_OWN, 1, 4), (REDUCE_NEAR, 0, 1), (REDUCE_NEAR, 2, 1),
-    (REDUCE_NEAR, 0, 2), (REDUCE_NEAR, 2, 0), (REDUCE_NEAR, 0, 3), (REDUCE_NEAR, 2, 3),
-    (FINISH_OWN, 1, 1), (REDUCE_NEAR, 2, 2), (FINISH_OWN, 1, 3), (FINISH_OWN, 1, 0),
-    (FINISH_OWN, 1, 2),
+    (SEND_CORE,), (SEND_Z, 6, BEHIND), (SEND_Z, 4, AHEAD), (SEND_Z, 4, BEHIND),
+    (SEND_Z, 7, AHEAD), (CROSS_FIRST,), (SEND_Y, 1), (SEND_Z, 6, AHEAD), (SEND_Y, 3),
+    (SEND_Z, 5, BEHIND), (SEND_Z, 5, AHEAD), (RELAY_OWN, 0, 4), (RELAY_OWN, 2, 4), (PASS_CORE, 7),
+    (SEND_Z, 0, AHEAD), (PASS_Z, 7), (SEND_Z, 7, BEHIND), (SEND_Y, 0), (PASS_CORE, 1),
+    (SEND_Z, 1, BEHIND), (RELAY_OWN, 2, 6), (PASS_CORE, 3), (RELAY_OWN, 0, 6), (RELAY_OWN, 0, 5),
+    (SEND_Y, 4), (RELAY_CORE, 0, 4), (RELAY_SIDE, 0, 7), (SEND_Y, 2), (RELAY_OWN, 3, 4),
+    (RELAY_CORE, 2, 4), (RELAY_OWN, 2, 5), (SEND_Z, 3, BEHIND), (RELAY_OWN, 2, 7),
+    (SEND_Z, 0, BEHIND), (RELAY_OWN, 2, 0), (SEND_Z, 2, BEHIND), (PASS_CORE, 0),
+    (RELAY_OWN, 0, 3), (SEND_Z, 2, AHEAD), (RELAY_CORE, 2, 6), (RELAY_SIDE, 2, 7),
+    (RELAY_OWN, 3, 6), (RELAY_CORE, 0, 6), (RELAY_OWN, 0, 1), (RELAY_OWN, 3, 5),
+    (RELAY_OWN, 0, 0), (RELAY_CORE, 0, 5), (RELAY_SIDE, 3, 7), (PASS_CORE, 4), (RELAY_OWN, 0, 2),
+    (PASS_CORE, 2), (RELAY_OWN, 3, 3), (STEP, 0, 0), (RELAY_OWN, 0, 7), (STEP, 0, 1),
+    (STEP, 0, 2), (STEP, 0, 3), (RELAY_OWN, 3, 0), (RELAY_CORE, 2, 0), (STEP, 0, 4), (STEP, 0, 5),
+    (SEND_Z, 3, AHEAD), (RELAY_CORE, 0, 3), (SEND_Z, 1, AHEAD), (STEP, 1, 0), (STEP, 1, 1),
+    (CROSS, 1, 3), (CROSS, 1, 0), (RELAY_OWN, 3, 7), (SEND_Y, 6), (CROSS, 1, 1),
+    (RELAY_CORE, 3, 6), (STEP, 1, 2), (RELAY_OWN, 3, 1), (STEP, 1, 3), (STEP, 1, 4),
+    (RELAY_CORE, 3, 5), (RELAY_OWN, 3, 2), (STEP, 1, 5), (RELAY_OWN, 2, 3), (RELAY_CORE, 3, 4),
+    (CROSS, 1, 2), (RELAY_CORE, 2, 5), (RELAY_OWN, 2, 2), (RELAY_OWN, 2, 1), (RELAY_CORE, 0, 1),
+    (SEND_Y, 5), (RELAY_CORE, 0, 0), (CROSS, 0, 4), (STEP, 2, 0), (STEP, 2, 1),
+    (RELAY_CORE, 3, 3), (STEP, 2, 2), (STEP, 2, 3), (RELAY_CORE, 3, 0), (STEP, 2, 4),
+    (STEP, 2, 5), (STEP, 3, 0), (STEP, 3, 1), (STEP, 3, 2), (STEP, 3, 3), (STEP, 3, 4),
+    (STEP, 3, 5), (RELAY_CORE, 0, 2), (PASS_CORE, 6), (CROSS, 3, 4), (REDUCE_FAR, 2, 7),
+    (REDUCE_FAR, 2, 6), (REDUCE_FAR, 2, 5), (RELAY_CORE, 3, 1), (CROSS, 2, 4),
+    (REDUCE_SIDE, 2, 5), (REDUCE_SIDE, 2, 7), (RELAY_CORE, 3, 2), (REDUCE_SIDE, 2, 6),
+    (STEP, 4, 0), (STEP, 4, 1), (STEP, 4, 2), (STEP, 4, 3), (STEP, 4, 4), (REDUCE_FAR, 3, 7),
+    (RELAY_CORE, 2, 2), (STEP, 4, 5), (STEP, 5, 0), (STEP, 5, 1), (CROSS, 3, 2),
+    (REDUCE_SIDE, 3, 6), (STEP, 5, 2), (STEP, 5, 3), (REDUCE_SIDE, 3, 5), (STEP, 5, 4),
+    (STEP, 5, 5), (REDUCE_FAR, 0, 7), (REDUCE_NEAR, 3, 4), (RELAY_CORE, 2, 1), (REDUCE_FAR, 3, 6),
+    (CROSS, 3, 3), (CROSS, 3, 0), (RELAY_CORE, 2, 3), (PASS_CORE, 5), (REDUCE_SIDE, 3, 7),
+    (CROSS, 3, 1), (REDUCE_SIDE, 0, 6), (REDUCE_NEAR, 2, 4), (REDUCE_FAR, 3, 5), (CROSS, 0, 2),
+    (CROSS, 0, 3), (CROSS, 0, 1), (CROSS, 0, 0), (STEP, 6, 0), (STEP, 6, 1), (STEP, 6, 2),
+    (REDUCE_NEAR, 0, 4), (STEP, 6, 3), (STEP, 6, 4), (STEP, 6, 5), (STEP, 7, 0),
+    (REDUCE_SIDE, 0, 7), (STEP, 7, 1), (CROSS, 2, 3), (CROSS, 2, 0), (STEP, 7, 2),
+    (REDUCE_NEAR, 3, 0), (STEP, 7, 3), (REDUCE_FAR, 0, 5), (STEP, 7, 4), (REDUCE_NEAR, 3, 2),
+    (STEP, 7, 5), (REDUCE_SIDE, 0, 5), (CROSS, 2, 2), (CROSS, 2, 1), (REDUCE_FAR, 0, 6),
+    (REDUCE_NEAR, 3, 1), (FINISH_SIDE, 1, 6), (CROSS, 1, 4), (FINISH_SIDE, 1, 7),
+    (FINISH_SIDE, 1, 5), (REDUCE_NEAR, 0, 0), (REDUCE_NEAR, 3, 3), (REDUCE_NEAR, 0, 2),
+    (REDUCE_NEAR, 2, 3), (REDUCE_NEAR, 0, 1), (REDUCE_NEAR, 0, 3), (REDUCE_NEAR, 2, 2),
+    (REDUCE_NEAR, 2, 0), (FINISH_OWN, 1, 3), (REDUCE_NEAR, 2, 1), (FINISH_OWN, 1, 6),
+    (FINISH_OWN, 1, 2), (FINISH_OWN, 1, 4), (FINISH_OWN, 1, 0), (FINISH_OWN, 1, 7),
+    (FINISH_OWN, 1, 1), (FINISH_OWN, 1, 5),
 )
 ROOM = 56 * 2**20
 
@@ -251,6 +252,7 @@
         if task[2] == 0:
             p, h = UNITS[q][task[1]]
             half = range(CHUNKS // 2, CHUNKS) if h == 0 else range(CHUNKS // 2)
+            half = {*half, TABLE_WITH}
             keys = [(core, p, k) for core in (CORE_OWN, CORE_SIDE) for k in half]
             keys += [(FROM_Y, p, k) for k in half if p == q or k < NEAR_IN]
             if p != q:
@@ -264,8 +266,8 @@
 
 def fused(
     n, hot, part, tok, routes, pick, gts, wg_in, wu_in, wd_in, hg_in, hu_in, hd_in, out,
-    xs, keep, sc, rc, sy, ry, sz, rz, wg, wu, wd, wh, hid, hhid, cs, ct, gw,
-    wsem, tsem, cts, ctr, up_s, down_s, z_r, y_s, y_r, c_s, c_r,
+    xs, keep, sc, rc, sy, ry, sz, rz, wg, wu, wd, wh, hid, hhid, table, gw,
+    wsem, tsem, tu_s, td_s, tz_r, ty_s, ty_r, tc_s, tc_r, up_s, down_s, z_r, y_s, y_r, c_s, c_r,
     rc_s, rc_r, ry_s, ry_r, rz_s, rz_r,
 ):
     nz = n // 4
@@ -317,14 +319,21 @@
     first.start()
     barrier = pltpu.get_barrier_semaphore()
 
-    @pl.loop(1, n)
-    def _(i):
+    def greet(device):
         pl.semaphore_signal(
-            barrier, inc=1, device_id={"expert": lax.rem(me + i, n)},
+            barrier, inc=1, device_id={"expert": device},
             device_id_type=pl.DeviceIdType.MESH,
         )
 
-    ct[...] = jnp.zeros_like(ct)
+    greet(peer_c)
+    greet(peer_y)
+    greet(ahead)
+
+    @pl.when(jnp.logical_not(outer))
+    def _():
+        greet(behind)
+
+    table[me] = jnp.zeros(table.shape[1:], jnp.float32)
     micros = gts.shape[0]
 
     def joined(parts):
@@ -344,19 +353,29 @@
         return sum(jnp.where(route == e, weight, 0.0) for route, weight in named)
 
     for e in range(n):
-        ct[e, 0:1, :] = row(e)
-        for h in range(hot):
-            ct[e, 1 + h : 2 + h, :] = jnp.where(chosen == h, warm_row, 0.0)
-
-    cs[me] = ct[me]
+        table[me, e : e + 1, :] = row(e)
+    for h in range(hot):
+        table[me, n + h : n + h + 1, :] = jnp.where(chosen == h, warm_row, 0.0)
+
     first.wait()
     for load in loads:
         load.start()
-    pl.semaphore_wait(barrier, n - 1)
-
-    def ct_copy(i):
-        peer = lax.rem(me + i, n)
-        return remote(ct.at[peer], cs.at[me], cts.at[i], ctr.at[me], peer)
+    pl.semaphore_wait(barrier, jnp.where(outer, 3, 4))
+
+    def table_z(way, p):
+        ref = table.at[plane(p) * 4 + own]
+        send = tu_s if way == AHEAD else td_s
+        return remote(
+            ref, ref, send.at[plane(p)], tz_r.at[plane(p)], ahead if way == AHEAD else behind
+        )
+
+    def table_y(p):
+        ref = table.at[plane(p) * 4 + own]
+        return remote(ref, ref, ty_s.at[plane(p)], ty_r.at[plane(p)], peer_y)
+
+    def table_c(p, which):
+        ref = table.at[plane(p) * 4 + (own, side)[which]]
+        return remote(ref, ref, tc_s.at[plane(p), which], tc_r.at[plane(p), which], peer_c)
 
     def go_z(way, p, slot, k):
         at = k if slot is own else CHUNKS + k - NEAR_IN
@@ -406,14 +425,21 @@
 
     def await_event(q, key):
         name, p, k, *rest = key
+        tabled = k == TABLE_WITH
         if name == OWN:
+            if tabled:
+                table_z(AHEAD, p).wait_recv()
             go_z(AHEAD, p, own, k).wait_recv()
         elif name == SIDE:
             go_z(AHEAD, p, side, k).wait_recv()
         elif name == FROM_Y:
+            if tabled:
+                table_y(p).wait_recv()
             ref = xs.at[plane(p), side, span(k)]
             remote(ref, ref, y_s.at[plane(p), k], y_r.at[plane(p), k], peer_y).wait_recv()
         elif name in (CORE_OWN, CORE_SIDE):
+            if tabled:
+                table_c(p, int(name == CORE_SIDE)).wait_recv()
             go_c(p, int(name == CORE_SIDE), k).wait_recv()
         elif name in (SHARE_OWN, SHARE_SIDE):
             share(plane(p), k, y if name == SHARE_OWN else 1 - y, rest[0]).wait_recv()
@@ -444,19 +470,31 @@
                 if k >= NEAR_IN:
                     go_y(q, k).start()
         elif name == SEND_Z:
+            if at[0] == TABLE_WITH:
+                table_z(at[1], q).start()
             go_z(at[1], q, own, at[0]).start()
         elif name == SEND_CORE:
+            table_c(q, 0).start()
             for k in range(CHUNKS):
                 go_c(q, 0, k).start()
         elif name == PASS_Z:
             for way in ways(q, q):
                 go_z(way, q, side, at[0]).start()
         elif name == SEND_Y:
+            if at[0] == TABLE_WITH:
+                table_y(q).start()
             go_y(q, at[0]).start()
         elif name == PASS_CORE:
+            if at[0] == TABLE_WITH:
+                table_c(q, 1).start()
             go_c(q, 1, at[0]).start()
         elif name == RELAY_OWN:
             p, k = at
+            if k == TABLE_WITH:
+                for way in ways(q, p):
+                    table_z(way, p).start()
+                table_y(p).start()
+                table_c(p, 0).start()
             for way in ways(q, p):
                 go_z(way, p, own, k).start()
             if k < NEAR_IN:
@@ -468,6 +506,8 @@
                 go_z(way, p, side, k).start()
             go_c(p, 1, k).start()
         elif name == RELAY_CORE:
+            if at[1] == TABLE_WITH:
+                table_c(at[0], 1).start()
             go_c(at[0], 1, at[1]).start()
         else:
             p, k = at
@@ -533,7 +573,7 @@
         ]
         return jnp.where(outer, *found)
 
-    def take_tables():
+    def take_weights():
         if pad > hot * part:
             for t in range(3):
                 blank = wh.at[pl.ds(t * pad + hot * part, pad - hot * part)]
@@ -542,26 +582,11 @@
         for load in loads:
             load.wait()
 
-        @pl.loop(1, n)
-        def _(i):
-            other = lax.rem(me + i, n)
-            remote(
-                ct.at[other], cs.at[other], cts.at[i], ctr.at[other], other
-            ).wait_recv()
-
-        @pl.loop(0, n)
-        def _(e):
-            gw[e] = jnp.transpose(cs[e])
-
     def start(q):
         for keys, task in plans[q][-1, STEPS - 1]:
             if task is None:
-                take_tables()
+                take_weights()
             perform(q, [(keys, task)])
-
-    @pl.loop(1, n)
-    def _(i):
-        ct_copy(i).start()
 
     by_class(start)
 
@@ -574,9 +599,15 @@
         def block():
             return xs[here, :, lines, :].reshape(4 * half, model)
 
+        for j in range(4):
+            given = [table[here * 4 + j, pl.ds(me, 1), :]]
+            given += [table[here * 4 + j, n + i : n + i + 1, :] for i in range(hot)]
+            given.append(jnp.zeros((8 - len(given), rows), jnp.float32))
+            gw[j] = jnp.transpose(jnp.concatenate(given, axis=0))
+
         def columns(which):
             return jnp.concatenate(
-                [gw[here * 4 + j, lines, which : which + 1] for j in range(4)], axis=0
+                [gw[j, lines, which : which + 1] for j in range(4)], axis=0
             )
 
         for i in range(3):
@@ -619,12 +650,13 @@
 
     by_class(lambda q: perform(q, plans[q][count - 1, STEPS - 1]))
 
-    @pl.loop(1, n)
-    def _(i):
-        ct_copy(i).wait_send()
-
     def settle(q):
         for p in range(nz):
+            for way in ways(q, p):
+                table_z(way, p).wait_send()
+            table_y(p).wait_send()
+            table_c(p, 0).wait_send()
+            table_c(p, 1).wait_send()
             for k in range(CHUNKS):
                 for way in ways(q, p):
                     go_z(way, p, own, k).wait_send()
@@ -668,10 +700,10 @@
         pltpu.VMEM((3 * pad, model), half),
         pltpu.VMEM((2 * rows, units), half),
         pltpu.VMEM((2 * rows, pad), half),
-        pltpu.VMEM((n, 8, rows), full),
-        pltpu.VMEM((n, 8, rows), full),
-        pltpu.VMEM((n, rows, 8), full),
-        dma((3 + 3 * hot,)), dma, dma((n,)), dma((n,)),
+        pltpu.VMEM((n, -(-(n + hot) // 8) * 8, rows), full),
+        pltpu.VMEM((4, rows, 8), full),
+        dma((3 + 3 * hot,)), dma, dma((nz,)), dma((nz,)), dma((nz,)),
+        dma((nz,)), dma((nz,)), dma((nz, 2)), dma((nz, 2)),
         dma((nz, gathers)), dma((nz, gathers)), dma((nz, gathers)),
         dma((nz, CHUNKS)), dma((nz, CHUNKS)), dma((nz, 2, CHUNKS)), dma((nz, 2, CHUNKS)),
         dma((nz, 2, 2, 2)), dma((nz, 2, 2, 2)),

time: 95.1 us -> 91.8 us (0.965)
  Pallas kernels: 92.9 us -> 89.7 us
    pallas_call x1, Pallas kernels: 92.9 us -> 89.7 us  [shards(): pl.pallas_call(functools.partial(fused, n, hot, part), out_shape=jax.Shap...]
where the time goes in v3:
time: 91.8 us; the launch traced here: 91.6 us
  Pallas kernels  89.7 us (98%)
  local copies, waits for them, and re-layouts  1.88 us (2%)
    pallas_call x1, Pallas kernels, shards(): pl.pallas_call(functools.partial(fused, n, hot, part), out_shape=jax.Shap...  89.7 us
    unnamed x1, local copies, waits for them, and re-layouts  1.88 us

profile of v3, /device:TPU:0, one launch (start us, length us, event | category | flops | bytes accessed | tf_op | source)
XLA Modules:
  0.0 91.6 jit_solution(11135300866244466936)
XLA Ops:
  0.0 89.7 %shard_map.100 = bf16[128,2048]{1,0:T(8,128)(2,1)} custom-call(bf16[128,2048]{1,0:T(8,128)(2,1)} %bitcast.14, s32[7,2,64]{2,1,0:T(2,128)} %bitcast.19, s32[2,64]{1,0:T(2,128)} %pick.1, f32[2,8,64]{2,1,0:T(8,128)} %bitcast.18, bf16[2048,768]{1,0:T(8,128)(2,1)} %bitcast.10, bf16[2048,768]{1,0:T(8,128)(2,1)} %bitcast.11, bf16[768,2048]{1,0:T(8,128)(2,1)} %bitcast.12, ...), custom_call_target="tpu_custom_call" | custom-call | tf_op jit(solution)/shard_map/pallas_call | solution.py:728
  89.7 1.9 %copy.12 = bf16[2,64,2048]{2,1,0:T(8,128)(2,1)} copy(bf16[2,64,2048]{2,1,0:T(8,128)(2,1)} %bitcast.13) | data formatting | bytes 1048576

commit v4 on v3

--- a/solution.py
+++ b/solution.py
@@ -109,97 +109,98 @@
 AHEAD, BEHIND = range(2)
 CHUNKS = 8
 NEAR_IN = 7
-NEAR_OUT = 5
-HIGH = (4, 6, 7, 5)
-LOW = (2, 1, 3, 0)
+NEAR_OUT = 4
+HIGH = (7, 6, 5, 4)
+LOW = (3, 2, 1, 0)
 STEPS = 6
 TABLE_WITH = 4
 UNITS = (
-    ((1, 0), (0, 0), (2, 0), (3, 0), (1, 1), (3, 1), (2, 1), (0, 1)),
-    ((1, 1), (0, 0), (3, 0), (2, 0), (3, 1), (0, 1), (2, 1), (1, 0)),
+    ((1, 0), (2, 0), (0, 1), (3, 0), (3, 1), (2, 1), (1, 1), (0, 0)),
+    ((1, 0), (2, 0), (0, 0), (3, 0), (0, 1), (3, 1), (2, 1), (1, 1)),
 )
 OUTER = (
-    (SEND_Y, 1), (SEND_CORE,), (SEND_Z, 4, AHEAD), (CROSS_FIRST,), (SEND_Z, 7, AHEAD),
-    (SEND_Y, 2), (SEND_Z, 6, AHEAD), (SEND_Y, 3), (PASS_CORE, 1), (SEND_Z, 5, AHEAD),
-    (RELAY_OWN, 1, 6), (PASS_Z, 7), (PASS_CORE, 7), (RELAY_OWN, 1, 4), (PASS_CORE, 2),
-    (SEND_Z, 2, AHEAD), (RELAY_OWN, 1, 5), (SEND_Z, 3, AHEAD), (SEND_Y, 4), (PASS_CORE, 3),
-    (SEND_Y, 6), (RELAY_OWN, 2, 4), (RELAY_CORE, 1, 6), (RELAY_SIDE, 1, 7), (RELAY_CORE, 1, 4),
-    (SEND_Z, 1, AHEAD), (RELAY_OWN, 1, 7), (SEND_Z, 0, AHEAD), (RELAY_CORE, 1, 5),
-    (RELAY_OWN, 1, 1), (SEND_Y, 5), (STEP, 0, 0), (PASS_CORE, 4), (RELAY_OWN, 2, 6), (STEP, 0, 1),
-    (STEP, 0, 2), (STEP, 0, 3), (STEP, 0, 4), (RELAY_OWN, 3, 4), (STEP, 0, 5), (PASS_CORE, 6),
-    (RELAY_OWN, 2, 5), (RELAY_CORE, 1, 1), (RELAY_OWN, 1, 3), (RELAY_CORE, 2, 4),
-    (REDUCE_FAR, 1, 7), (REDUCE_FAR, 1, 5), (REDUCE_FAR, 1, 6), (REDUCE_SIDE, 1, 5),
-    (REDUCE_SIDE, 1, 6), (REDUCE_SIDE, 1, 7), (PASS_CORE, 5), (CROSS, 1, 4), (RELAY_OWN, 2, 7),
-    (STEP, 1, 0), (RELAY_CORE, 2, 6), (RELAY_OWN, 1, 0), (STEP, 1, 1), (RELAY_OWN, 2, 0),
-    (RELAY_CORE, 3, 4), (STEP, 1, 2), (STEP, 1, 3), (RELAY_OWN, 1, 2), (RELAY_CORE, 2, 5),
-    (STEP, 1, 4), (STEP, 1, 5), (RELAY_SIDE, 2, 7), (RELAY_CORE, 1, 3), (REDUCE_NEAR, 1, 4),
-    (CROSS, 0, 4), (RELAY_OWN, 3, 6), (STEP, 2, 0), (STEP, 2, 1), (RELAY_OWN, 3, 5), (STEP, 2, 2),
-    (RELAY_SIDE, 3, 7), (STEP, 2, 3), (STEP, 2, 4), (STEP, 2, 5), (RELAY_CORE, 1, 2),
-    (RELAY_CORE, 2, 0), (RELAY_OWN, 3, 3), (RELAY_CORE, 1, 0), (SEND_Y, 0), (RELAY_OWN, 3, 0),
-    (REDUCE_FAR, 2, 7), (REDUCE_FAR, 2, 5), (REDUCE_FAR, 2, 6), (REDUCE_SIDE, 2, 5),
-    (REDUCE_SIDE, 2, 7), (REDUCE_SIDE, 2, 6), (CROSS, 2, 4), (RELAY_CORE, 3, 6),
-    (RELAY_OWN, 3, 7), (RELAY_CORE, 3, 5), (RELAY_OWN, 3, 1), (STEP, 3, 0), (RELAY_CORE, 3, 3),
-    (RELAY_OWN, 3, 2), (STEP, 3, 1), (RELAY_OWN, 2, 3), (PASS_CORE, 0), (STEP, 3, 2),
-    (STEP, 3, 3), (RELAY_CORE, 3, 0), (STEP, 3, 4), (STEP, 3, 5), (REDUCE_NEAR, 2, 4),
-    (RELAY_OWN, 2, 1), (RELAY_OWN, 2, 2), (STEP, 4, 0), (REDUCE_FAR, 3, 6), (REDUCE_FAR, 3, 7),
-    (STEP, 4, 1), (REDUCE_SIDE, 3, 7), (REDUCE_SIDE, 3, 6), (RELAY_CORE, 3, 1),
-    (REDUCE_SIDE, 3, 5), (CROSS, 3, 4), (STEP, 4, 2), (RELAY_CORE, 3, 2), (STEP, 4, 3),
-    (STEP, 4, 4), (RELAY_CORE, 2, 3), (STEP, 4, 5), (STEP, 5, 0), (STEP, 5, 1), (CROSS, 1, 3),
-    (CROSS, 1, 2), (CROSS, 1, 1), (STEP, 5, 2), (STEP, 5, 3), (REDUCE_NEAR, 3, 4), (STEP, 5, 4),
-    (STEP, 5, 5), (RELAY_CORE, 2, 2), (REDUCE_FAR, 3, 5), (REDUCE_NEAR, 1, 3), (CROSS, 1, 0),
-    (RELAY_CORE, 2, 1), (CROSS, 3, 3), (CROSS, 3, 0), (CROSS, 3, 2), (CROSS, 3, 1),
-    (REDUCE_NEAR, 1, 2), (STEP, 6, 0), (STEP, 6, 1), (REDUCE_NEAR, 1, 1), (STEP, 6, 2),
-    (REDUCE_NEAR, 1, 0), (STEP, 6, 3), (STEP, 6, 4), (STEP, 6, 5), (STEP, 7, 0),
-    (FINISH_SIDE, 0, 6), (REDUCE_NEAR, 3, 0), (STEP, 7, 1), (CROSS, 2, 3), (CROSS, 2, 2),
-    (STEP, 7, 2), (REDUCE_NEAR, 3, 2), (FINISH_OWN, 0, 4), (STEP, 7, 3), (STEP, 7, 4),
-    (REDUCE_NEAR, 3, 1), (STEP, 7, 5), (CROSS, 2, 0), (CROSS, 2, 1), (REDUCE_NEAR, 3, 3),
-    (FINISH_SIDE, 0, 7), (CROSS, 0, 0), (CROSS, 0, 3), (CROSS, 0, 2), (CROSS, 0, 1),
-    (REDUCE_NEAR, 2, 3), (REDUCE_NEAR, 2, 2), (REDUCE_NEAR, 2, 0), (FINISH_SIDE, 0, 5),
-    (REDUCE_NEAR, 2, 1), (FINISH_OWN, 0, 6), (FINISH_OWN, 0, 7), (FINISH_OWN, 0, 0),
-    (FINISH_OWN, 0, 2), (FINISH_OWN, 0, 3), (FINISH_OWN, 0, 1), (FINISH_OWN, 0, 5),
+    (SEND_Z, 5, AHEAD), (SEND_Y, 1), (SEND_CORE,), (SEND_Z, 7, AHEAD), (SEND_Y, 6),
+    (CROSS_FIRST,), (RELAY_OWN, 1, 6), (PASS_CORE, 1), (RELAY_OWN, 1, 4), (SEND_Z, 4, AHEAD),
+    (PASS_CORE, 6), (SEND_Z, 6, AHEAD), (RELAY_OWN, 1, 5), (PASS_Z, 7), (SEND_Z, 3, AHEAD),
+    (SEND_Z, 0, AHEAD), (SEND_Z, 2, AHEAD), (PASS_CORE, 7), (RELAY_OWN, 1, 7), (RELAY_CORE, 1, 6),
+    (SEND_Y, 4), (SEND_Y, 0), (SEND_Y, 2), (SEND_Z, 1, AHEAD), (RELAY_OWN, 2, 6),
+    (RELAY_CORE, 1, 4), (RELAY_SIDE, 1, 7), (RELAY_CORE, 1, 5), (STEP, 0, 0), (RELAY_OWN, 2, 4),
+    (STEP, 0, 1), (RELAY_OWN, 2, 5), (STEP, 0, 2), (STEP, 0, 3), (RELAY_OWN, 3, 5), (SEND_Y, 3),
+    (STEP, 0, 4), (STEP, 0, 5), (PASS_CORE, 2), (PASS_CORE, 4), (PASS_CORE, 0),
+    (RELAY_CORE, 2, 6), (RELAY_SIDE, 2, 7), (RELAY_OWN, 3, 7), (REDUCE_FAR, 1, 5),
+    (REDUCE_FAR, 1, 6), (REDUCE_FAR, 1, 4), (REDUCE_SIDE, 1, 7), (REDUCE_SIDE, 1, 6),
+    (RELAY_CORE, 2, 4), (REDUCE_SIDE, 1, 4), (REDUCE_SIDE, 1, 5), (REDUCE_FAR, 1, 7),
+    (RELAY_OWN, 2, 7), (RELAY_CORE, 2, 5), (RELAY_OWN, 3, 4), (SEND_Y, 5), (STEP, 1, 0),
+    (RELAY_CORE, 3, 5), (RELAY_OWN, 2, 2), (STEP, 1, 1), (STEP, 1, 2), (RELAY_OWN, 1, 2),
+    (STEP, 1, 3), (STEP, 1, 4), (STEP, 1, 5), (PASS_CORE, 3), (PASS_CORE, 5), (RELAY_CORE, 3, 4),
+    (RELAY_OWN, 3, 6), (RELAY_OWN, 2, 1), (RELAY_CORE, 2, 2), (RELAY_OWN, 3, 0),
+    (REDUCE_FAR, 2, 4), (REDUCE_FAR, 2, 5), (REDUCE_FAR, 2, 7), (REDUCE_SIDE, 2, 6),
+    (REDUCE_SIDE, 2, 5), (REDUCE_SIDE, 2, 7), (REDUCE_SIDE, 2, 4), (STEP, 2, 0),
+    (RELAY_CORE, 1, 2), (RELAY_OWN, 1, 0), (STEP, 2, 1), (STEP, 2, 2), (RELAY_CORE, 3, 6),
+    (RELAY_SIDE, 3, 7), (STEP, 2, 3), (RELAY_OWN, 3, 2), (STEP, 2, 4), (STEP, 2, 5),
+    (RELAY_OWN, 3, 3), (STEP, 3, 0), (RELAY_OWN, 3, 1), (STEP, 3, 1), (STEP, 3, 2),
+    (RELAY_OWN, 1, 1), (RELAY_CORE, 3, 2), (STEP, 3, 3), (STEP, 3, 4), (RELAY_OWN, 2, 0),
+    (RELAY_CORE, 3, 3), (STEP, 3, 5), (RELAY_CORE, 3, 1), (RELAY_OWN, 2, 3), (RELAY_CORE, 3, 0),
+    (CROSS, 0, 2), (RELAY_CORE, 2, 1), (CROSS, 0, 1), (REDUCE_FAR, 2, 6), (CROSS, 0, 0),
+    (CROSS, 0, 3), (RELAY_CORE, 1, 0), (REDUCE_FAR, 3, 7), (REDUCE_FAR, 3, 4), (RELAY_OWN, 1, 3),
+    (REDUCE_FAR, 3, 5), (REDUCE_SIDE, 3, 4), (RELAY_CORE, 1, 1), (REDUCE_SIDE, 3, 6),
+    (REDUCE_SIDE, 3, 7), (STEP, 4, 0), (STEP, 4, 1), (RELAY_CORE, 2, 0), (STEP, 4, 2),
+    (RELAY_CORE, 2, 3), (STEP, 4, 3), (STEP, 4, 4), (STEP, 4, 5), (STEP, 5, 0), (STEP, 5, 1),
+    (CROSS, 3, 2), (CROSS, 3, 0), (CROSS, 3, 3), (STEP, 5, 2), (STEP, 5, 3), (STEP, 5, 4),
+    (RELAY_CORE, 1, 3), (STEP, 5, 5), (CROSS, 3, 1), (REDUCE_SIDE, 3, 5), (REDUCE_FAR, 3, 6),
+    (REDUCE_NEAR, 3, 2), (STEP, 6, 0), (CROSS, 2, 3), (CROSS, 2, 2), (CROSS, 2, 1),
+    (REDUCE_NEAR, 3, 0), (CROSS, 2, 0), (STEP, 6, 1), (STEP, 6, 2), (REDUCE_NEAR, 3, 3),
+    (STEP, 6, 3), (STEP, 6, 4), (REDUCE_NEAR, 3, 1), (STEP, 6, 5), (REDUCE_NEAR, 2, 3),
+    (STEP, 7, 0), (STEP, 7, 1), (CROSS, 1, 0), (CROSS, 1, 1), (CROSS, 1, 3), (CROSS, 1, 2),
+    (REDUCE_NEAR, 2, 1), (STEP, 7, 2), (STEP, 7, 3), (REDUCE_NEAR, 2, 0), (STEP, 7, 4),
+    (STEP, 7, 5), (REDUCE_NEAR, 2, 2), (REDUCE_NEAR, 1, 0), (FINISH_SIDE, 0, 5),
+    (REDUCE_NEAR, 1, 1), (FINISH_SIDE, 0, 4), (FINISH_SIDE, 0, 7), (FINISH_SIDE, 0, 6),
+    (REDUCE_NEAR, 1, 3), (FINISH_OWN, 0, 2), (REDUCE_NEAR, 1, 2), (FINISH_OWN, 0, 0),
+    (FINISH_OWN, 0, 5), (FINISH_OWN, 0, 3), (FINISH_OWN, 0, 4), (FINISH_OWN, 0, 1),
+    (FINISH_OWN, 0, 7), (FINISH_OWN, 0, 6),
 )
 INNER = (
-    (SEND_CORE,), (SEND_Z, 6, BEHIND), (SEND_Z, 4, AHEAD), (SEND_Z, 4, BEHIND),
-    (SEND_Z, 7, AHEAD), (CROSS_FIRST,), (SEND_Y, 1), (SEND_Z, 6, AHEAD), (SEND_Y, 3),
-    (SEND_Z, 5, BEHIND), (SEND_Z, 5, AHEAD), (RELAY_OWN, 0, 4), (RELAY_OWN, 2, 4), (PASS_CORE, 7),
-    (SEND_Z, 0, AHEAD), (PASS_Z, 7), (SEND_Z, 7, BEHIND), (SEND_Y, 0), (PASS_CORE, 1),
-    (SEND_Z, 1, BEHIND), (RELAY_OWN, 2, 6), (PASS_CORE, 3), (RELAY_OWN, 0, 6), (RELAY_OWN, 0, 5),
-    (SEND_Y, 4), (RELAY_CORE, 0, 4), (RELAY_SIDE, 0, 7), (SEND_Y, 2), (RELAY_OWN, 3, 4),
-    (RELAY_CORE, 2, 4), (RELAY_OWN, 2, 5), (SEND_Z, 3, BEHIND), (RELAY_OWN, 2, 7),
-    (SEND_Z, 0, BEHIND), (RELAY_OWN, 2, 0), (SEND_Z, 2, BEHIND), (PASS_CORE, 0),
-    (RELAY_OWN, 0, 3), (SEND_Z, 2, AHEAD), (RELAY_CORE, 2, 6), (RELAY_SIDE, 2, 7),
-    (RELAY_OWN, 3, 6), (RELAY_CORE, 0, 6), (RELAY_OWN, 0, 1), (RELAY_OWN, 3, 5),
-    (RELAY_OWN, 0, 0), (RELAY_CORE, 0, 5), (RELAY_SIDE, 3, 7), (PASS_CORE, 4), (RELAY_OWN, 0, 2),
-    (PASS_CORE, 2), (RELAY_OWN, 3, 3), (STEP, 0, 0), (RELAY_OWN, 0, 7), (STEP, 0, 1),
-    (STEP, 0, 2), (STEP, 0, 3), (RELAY_OWN, 3, 0), (RELAY_CORE, 2, 0), (STEP, 0, 4), (STEP, 0, 5),
-    (SEND_Z, 3, AHEAD), (RELAY_CORE, 0, 3), (SEND_Z, 1, AHEAD), (STEP, 1, 0), (STEP, 1, 1),
-    (CROSS, 1, 3), (CROSS, 1, 0), (RELAY_OWN, 3, 7), (SEND_Y, 6), (CROSS, 1, 1),
-    (RELAY_CORE, 3, 6), (STEP, 1, 2), (RELAY_OWN, 3, 1), (STEP, 1, 3), (STEP, 1, 4),
-    (RELAY_CORE, 3, 5), (RELAY_OWN, 3, 2), (STEP, 1, 5), (RELAY_OWN, 2, 3), (RELAY_CORE, 3, 4),
-    (CROSS, 1, 2), (RELAY_CORE, 2, 5), (RELAY_OWN, 2, 2), (RELAY_OWN, 2, 1), (RELAY_CORE, 0, 1),
-    (SEND_Y, 5), (RELAY_CORE, 0, 0), (CROSS, 0, 4), (STEP, 2, 0), (STEP, 2, 1),
-    (RELAY_CORE, 3, 3), (STEP, 2, 2), (STEP, 2, 3), (RELAY_CORE, 3, 0), (STEP, 2, 4),
-    (STEP, 2, 5), (STEP, 3, 0), (STEP, 3, 1), (STEP, 3, 2), (STEP, 3, 3), (STEP, 3, 4),
-    (STEP, 3, 5), (RELAY_CORE, 0, 2), (PASS_CORE, 6), (CROSS, 3, 4), (REDUCE_FAR, 2, 7),
-    (REDUCE_FAR, 2, 6), (REDUCE_FAR, 2, 5), (RELAY_CORE, 3, 1), (CROSS, 2, 4),
-    (REDUCE_SIDE, 2, 5), (REDUCE_SIDE, 2, 7), (RELAY_CORE, 3, 2), (REDUCE_SIDE, 2, 6),
-    (STEP, 4, 0), (STEP, 4, 1), (STEP, 4, 2), (STEP, 4, 3), (STEP, 4, 4), (REDUCE_FAR, 3, 7),
-    (RELAY_CORE, 2, 2), (STEP, 4, 5), (STEP, 5, 0), (STEP, 5, 1), (CROSS, 3, 2),
-    (REDUCE_SIDE, 3, 6), (STEP, 5, 2), (STEP, 5, 3), (REDUCE_SIDE, 3, 5), (STEP, 5, 4),
-    (STEP, 5, 5), (REDUCE_FAR, 0, 7), (REDUCE_NEAR, 3, 4), (RELAY_CORE, 2, 1), (REDUCE_FAR, 3, 6),
-    (CROSS, 3, 3), (CROSS, 3, 0), (RELAY_CORE, 2, 3), (PASS_CORE, 5), (REDUCE_SIDE, 3, 7),
-    (CROSS, 3, 1), (REDUCE_SIDE, 0, 6), (REDUCE_NEAR, 2, 4), (REDUCE_FAR, 3, 5), (CROSS, 0, 2),
-    (CROSS, 0, 3), (CROSS, 0, 1), (CROSS, 0, 0), (STEP, 6, 0), (STEP, 6, 1), (STEP, 6, 2),
-    (REDUCE_NEAR, 0, 4), (STEP, 6, 3), (STEP, 6, 4), (STEP, 6, 5), (STEP, 7, 0),
-    (REDUCE_SIDE, 0, 7), (STEP, 7, 1), (CROSS, 2, 3), (CROSS, 2, 0), (STEP, 7, 2),
-    (REDUCE_NEAR, 3, 0), (STEP, 7, 3), (REDUCE_FAR, 0, 5), (STEP, 7, 4), (REDUCE_NEAR, 3, 2),
-    (STEP, 7, 5), (REDUCE_SIDE, 0, 5), (CROSS, 2, 2), (CROSS, 2, 1), (REDUCE_FAR, 0, 6),
-    (REDUCE_NEAR, 3, 1), (FINISH_SIDE, 1, 6), (CROSS, 1, 4), (FINISH_SIDE, 1, 7),
-    (FINISH_SIDE, 1, 5), (REDUCE_NEAR, 0, 0), (REDUCE_NEAR, 3, 3), (REDUCE_NEAR, 0, 2),
-    (REDUCE_NEAR, 2, 3), (REDUCE_NEAR, 0, 1), (REDUCE_NEAR, 0, 3), (REDUCE_NEAR, 2, 2),
-    (REDUCE_NEAR, 2, 0), (FINISH_OWN, 1, 3), (REDUCE_NEAR, 2, 1), (FINISH_OWN, 1, 6),
-    (FINISH_OWN, 1, 2), (FINISH_OWN, 1, 4), (FINISH_OWN, 1, 0), (FINISH_OWN, 1, 7),
-    (FINISH_OWN, 1, 1), (FINISH_OWN, 1, 5),
+    (SEND_Z, 6, BEHIND), (SEND_Z, 6, AHEAD), (SEND_Z, 4, BEHIND), (SEND_CORE,),
+    (SEND_Z, 5, BEHIND), (CROSS_FIRST,), (SEND_Y, 4), (SEND_Y, 6), (SEND_Z, 4, AHEAD),
+    (SEND_Z, 5, AHEAD), (SEND_Y, 1), (SEND_Z, 7, BEHIND), (SEND_Y, 5), (RELAY_OWN, 0, 5),
+    (RELAY_OWN, 2, 6), (PASS_Z, 7), (SEND_Z, 2, AHEAD), (PASS_CORE, 7), (RELAY_OWN, 2, 4),
+    (RELAY_OWN, 0, 7), (PASS_CORE, 4), (RELAY_OWN, 2, 5), (PASS_CORE, 6), (SEND_Z, 7, AHEAD),
+    (RELAY_OWN, 3, 5), (PASS_CORE, 1), (RELAY_OWN, 0, 4), (RELAY_SIDE, 2, 7), (PASS_CORE, 5),
+    (RELAY_OWN, 0, 6), (STEP, 0, 0), (STEP, 0, 1), (RELAY_SIDE, 0, 7), (RELAY_OWN, 3, 7),
+    (STEP, 0, 2), (SEND_Z, 1, AHEAD), (STEP, 0, 3), (RELAY_OWN, 2, 7), (RELAY_CORE, 2, 4),
+    (STEP, 0, 4), (RELAY_OWN, 0, 0), (RELAY_OWN, 3, 4), (STEP, 0, 5), (RELAY_CORE, 2, 5),
+    (RELAY_OWN, 0, 2), (RELAY_CORE, 2, 6), (RELAY_OWN, 0, 3), (RELAY_CORE, 0, 5),
+    (RELAY_OWN, 2, 2), (SEND_Z, 2, BEHIND), (RELAY_OWN, 3, 6), (RELAY_CORE, 3, 5),
+    (RELAY_OWN, 0, 1), (SEND_Z, 3, AHEAD), (STEP, 1, 0), (RELAY_CORE, 0, 4), (STEP, 1, 1),
+    (RELAY_OWN, 2, 1), (STEP, 1, 2), (STEP, 1, 3), (RELAY_OWN, 3, 0), (STEP, 1, 4),
+    (SEND_Z, 0, AHEAD), (RELAY_CORE, 0, 0), (SEND_Z, 0, BEHIND), (STEP, 1, 5), (RELAY_CORE, 0, 6),
+    (RELAY_SIDE, 3, 7), (RELAY_CORE, 3, 4), (RELAY_OWN, 3, 2), (SEND_Y, 3), (RELAY_OWN, 3, 3),
+    (RELAY_CORE, 0, 2), (STEP, 2, 0), (RELAY_OWN, 3, 1), (STEP, 2, 1), (RELAY_CORE, 0, 3),
+    (STEP, 2, 2), (RELAY_CORE, 2, 2), (STEP, 2, 3), (SEND_Z, 1, BEHIND), (STEP, 2, 4),
+    (RELAY_CORE, 3, 6), (STEP, 2, 5), (RELAY_OWN, 2, 0), (SEND_Y, 0), (RELAY_OWN, 2, 3),
+    (SEND_Z, 3, BEHIND), (SEND_Y, 2), (RELAY_CORE, 0, 1), (STEP, 3, 0), (STEP, 3, 1),
+    (STEP, 3, 2), (STEP, 3, 3), (REDUCE_FAR, 2, 4), (STEP, 3, 4), (RELAY_CORE, 3, 2),
+    (STEP, 3, 5), (STEP, 4, 0), (REDUCE_FAR, 2, 7), (STEP, 4, 1), (REDUCE_SIDE, 2, 6),
+    (STEP, 4, 2), (RELAY_CORE, 3, 1), (STEP, 4, 3), (REDUCE_SIDE, 2, 5), (STEP, 4, 4),
+    (REDUCE_SIDE, 2, 7), (RELAY_CORE, 2, 0), (STEP, 4, 5), (PASS_CORE, 0), (REDUCE_FAR, 2, 5),
+    (RELAY_CORE, 3, 3), (PASS_CORE, 3), (RELAY_CORE, 3, 0), (RELAY_CORE, 2, 1),
+    (REDUCE_SIDE, 2, 4), (FINISH_SIDE, 1, 6), (CROSS, 0, 2), (RELAY_CORE, 2, 3), (CROSS, 0, 1),
+    (CROSS, 0, 3), (CROSS, 0, 0), (REDUCE_FAR, 2, 6), (STEP, 5, 0), (FINISH_SIDE, 1, 5),
+    (STEP, 5, 1), (FINISH_SIDE, 1, 7), (REDUCE_FAR, 3, 7), (STEP, 5, 2), (REDUCE_FAR, 3, 4),
+    (STEP, 5, 3), (STEP, 5, 4), (STEP, 5, 5), (REDUCE_SIDE, 3, 4), (STEP, 6, 0),
+    (REDUCE_FAR, 0, 7), (REDUCE_SIDE, 3, 6), (CROSS, 3, 0), (CROSS, 3, 2), (CROSS, 3, 1),
+    (STEP, 6, 1), (REDUCE_SIDE, 3, 7), (STEP, 6, 2), (STEP, 6, 3), (REDUCE_SIDE, 0, 4),
+    (STEP, 6, 4), (STEP, 6, 5), (FINISH_OWN, 1, 7), (CROSS, 3, 3), (REDUCE_FAR, 0, 4),
+    (REDUCE_SIDE, 3, 5), (FINISH_OWN, 1, 6), (REDUCE_SIDE, 0, 7), (FINISH_SIDE, 1, 4),
+    (PASS_CORE, 2), (REDUCE_SIDE, 0, 6), (FINISH_OWN, 1, 5), (REDUCE_FAR, 3, 5), (CROSS, 2, 3),
+    (CROSS, 2, 1), (CROSS, 2, 0), (CROSS, 2, 2), (REDUCE_FAR, 3, 6), (STEP, 7, 0), (STEP, 7, 1),
+    (REDUCE_NEAR, 3, 2), (STEP, 7, 2), (REDUCE_NEAR, 3, 0), (REDUCE_SIDE, 0, 5), (STEP, 7, 3),
+    (REDUCE_FAR, 0, 5), (STEP, 7, 4), (REDUCE_NEAR, 3, 3), (STEP, 7, 5), (REDUCE_FAR, 0, 6),
+    (REDUCE_NEAR, 3, 1), (FINISH_OWN, 1, 4), (REDUCE_NEAR, 0, 2), (REDUCE_NEAR, 2, 3),
+    (CROSS, 1, 0), (CROSS, 1, 2), (CROSS, 1, 1), (CROSS, 1, 3), (REDUCE_NEAR, 0, 0),
+    (REDUCE_NEAR, 2, 1), (REDUCE_NEAR, 0, 3), (REDUCE_NEAR, 2, 0), (REDUCE_NEAR, 0, 1),
+    (REDUCE_NEAR, 2, 2), (FINISH_OWN, 1, 1), (FINISH_OWN, 1, 0), (FINISH_OWN, 1, 3),
+    (FINISH_OWN, 1, 2),
 )
 ROOM = 56 * 2**20
 

time: 91.8 us -> 85.6 us (0.932)
  Pallas kernels: 89.7 us -> 83.5 us
    pallas_call x1, Pallas kernels: 89.7 us -> 83.5 us  [shards(): pl.pallas_call(functools.partial(fused, n, hot, part), out_shape=jax.Shap...]
where the time goes in v4:
time: 85.6 us; the launch traced here: 85.4 us
  Pallas kernels  83.5 us (98%)
  local copies, waits for them, and re-layouts  1.88 us (2%)
    pallas_call x1, Pallas kernels, shards(): pl.pallas_call(functools.partial(fused, n, hot, part), out_shape=jax.Shap...  83.5 us
    unnamed x1, local copies, waits for them, and re-layouts  1.88 us

profile of v4, /device:TPU:0, one launch (start us, length us, event | category | flops | bytes accessed | tf_op | source)
XLA Modules:
  0.0 85.4 jit_solution(4545387523535246059)
XLA Ops:
  0.0 83.5 %shard_map.100 = bf16[128,2048]{1,0:T(8,128)(2,1)} custom-call(bf16[128,2048]{1,0:T(8,128)(2,1)} %bitcast.14, s32[7,2,64]{2,1,0:T(2,128)} %bitcast.19, s32[2,64]{1,0:T(2,128)} %pick.1, f32[2,8,64]{2,1,0:T(8,128)} %bitcast.18, bf16[2048,768]{1,0:T(8,128)(2,1)} %bitcast.10, bf16[2048,768]{1,0:T(8,128)(2,1)} %bitcast.11, bf16[768,2048]{1,0:T(8,128)(2,1)} %bitcast.12, ...), custom_call_target="tpu_custom_call" | custom-call | tf_op jit(solution)/shard_map/pallas_call | solution.py:729
  83.5 1.9 %copy.12 = bf16[2,64,2048]{2,1,0:T(8,128)(2,1)} copy(bf16[2,64,2048]{2,1,0:T(8,128)(2,1)} %bitcast.13) | data formatting | bytes 1048576

commit v5 on v4

--- a/solution.py
+++ b/solution.py
@@ -334,31 +334,6 @@
     def _():
         greet(behind)
 
-    table[me] = jnp.zeros(table.shape[1:], jnp.float32)
-    micros = gts.shape[0]
-
-    def joined(parts):
-        return jnp.concatenate(parts, axis=1)
-
-    warm_row = joined([gts[m, 0:1, :] for m in range(micros)])
-    chosen = joined([pick[m : m + 1, :] for m in range(micros)])
-    named = [
-        (
-            joined([routes[k, m : m + 1, :] for m in range(micros)]),
-            joined([gts[m, k + 1 : k + 2, :] for m in range(micros)]),
-        )
-        for k in range(routes.shape[0])
-    ]
-
-    def row(e):
-        return sum(jnp.where(route == e, weight, 0.0) for route, weight in named)
-
-    for e in range(n):
-        table[me, e : e + 1, :] = row(e)
-    for h in range(hot):
-        table[me, n + h : n + h + 1, :] = jnp.where(chosen == h, warm_row, 0.0)
-
-    first.wait()
     for load in loads:
         load.start()
     pl.semaphore_wait(barrier, jnp.where(outer, 3, 4))
@@ -378,23 +353,23 @@
         ref = table.at[plane(p) * 4 + (own, side)[which]]
         return remote(ref, ref, tc_s.at[plane(p), which], tc_r.at[plane(p), which], peer_c)
 
-    def go_z(way, p, slot, k):
+    def go_z(way, p, slot, k, fresh=False):
         at = k if slot is own else CHUNKS + k - NEAR_IN
         ref = xs.at[plane(p), slot, span(k)]
         send = up_s if way == AHEAD else down_s
         return remote(
-            ref, ref, send.at[plane(p), at], z_r.at[plane(p), at],
+            tok.at[span(k)] if fresh else ref, ref, send.at[plane(p), at], z_r.at[plane(p), at],
             ahead if way == AHEAD else behind,
         )
 
-    def go_y(p, k):
+    def go_y(p, k, fresh=False):
         ref = xs.at[plane(p), own, span(k)]
-        return remote(ref, ref, y_s.at[plane(p), k], y_r.at[plane(p), k], peer_y)
-
-    def go_c(p, which, k):
+        return remote(tok.at[span(k)] if fresh else ref, ref, y_s.at[plane(p), k], y_r.at[plane(p), k], peer_y)
+
+    def go_c(p, which, k, fresh=False):
         ref = xs.at[plane(p), (own, side)[which], span(k)]
         return remote(
-            ref, ref, c_s.at[plane(p), which, k], c_r.at[plane(p), which, k], peer_c
+            tok.at[span(k)] if fresh else ref, ref, c_s.at[plane(p), which, k], c_r.at[plane(p), which, k], peer_c
         )
 
     def share(at, h, j, t):
@@ -469,22 +444,22 @@
         if name == CROSS_FIRST:
             for k in HIGH + LOW:
                 if k >= NEAR_IN:
-                    go_y(q, k).start()
+                    go_y(q, k, fresh=True).start()
         elif name == SEND_Z:
             if at[0] == TABLE_WITH:
                 table_z(at[1], q).start()
-            go_z(at[1], q, own, at[0]).start()
+            go_z(at[1], q, own, at[0], fresh=True).start()
         elif name == SEND_CORE:
-            table_c(q, 0).start()
             for k in range(CHUNKS):
-                go_c(q, 0, k).start()
+                go_c(q, 0, k, fresh=True).start()
         elif name == PASS_Z:
             for way in ways(q, q):
                 go_z(way, q, side, at[0]).start()
         elif name == SEND_Y:
             if at[0] == TABLE_WITH:
                 table_y(q).start()
-            go_y(q, at[0]).start()
+                table_c(q, 0).start()
+            go_y(q, at[0], fresh=True).start()
         elif name == PASS_CORE:
             if at[0] == TABLE_WITH:
                 table_c(q, 1).start()
@@ -580,13 +555,43 @@
                 blank = wh.at[pl.ds(t * pad + hot * part, pad - hot * part)]
                 blank[...] = jnp.zeros_like(blank)
 
+        first.wait()
         for load in loads:
             load.wait()
 
+    def fill_table():
+        table[me] = jnp.zeros(table.shape[1:], jnp.float32)
+        micros = gts.shape[0]
+
+        def joined(parts):
+            return jnp.concatenate(parts, axis=1)
+
+        warm_row = joined([gts[m, 0:1, :] for m in range(micros)])
+        chosen = joined([pick[m : m + 1, :] for m in range(micros)])
+        named = [
+            (
+                joined([routes[k, m : m + 1, :] for m in range(micros)]),
+                joined([gts[m, k + 1 : k + 2, :] for m in range(micros)]),
+            )
+            for k in range(routes.shape[0])
+        ]
+
+        def row(e):
+            return sum(jnp.where(route == e, weight, 0.0) for route, weight in named)
+
+        for e in range(n):
+            table[me, e : e + 1, :] = row(e)
+        for h in range(hot):
+            table[me, n + h : n + h + 1, :] = jnp.where(chosen == h, warm_row, 0.0)
+
     def start(q):
+        filled = False
         for keys, task in plans[q][-1, STEPS - 1]:
             if task is None:
                 take_weights()
+            elif task[0] in (SEND_Z, SEND_Y) and task[1] == TABLE_WITH and not filled:
+                fill_table()
+                filled = True
             perform(q, [(keys, task)])
 
     by_class(start)
@@ -597,12 +602,14 @@
         h = picked(u, 1)
         lines = pl.ds(pl.multiple_of((1 - h) * half, half), half)
 
+        slots = (c, 2 + c, 1 - c, 3 - c)
+
         def block():
-            return xs[here, :, lines, :].reshape(4 * half, model)
-
-        for j in range(4):
-            given = [table[here * 4 + j, pl.ds(me, 1), :]]
-            given += [table[here * 4 + j, n + i : n + i + 1, :] for i in range(hot)]
+            return jnp.concatenate([xs[here, slot, lines, :] for slot in slots], axis=0)
+
+        for j, slot in enumerate(slots):
+            given = [table[here * 4 + slot, pl.ds(me, 1), :]]
+            given += [table[here * 4 + slot, n + i : n + i + 1, :] for i in range(hot)]
             given.append(jnp.zeros((8 - len(given), rows), jnp.float32))
             gw[j] = jnp.transpose(jnp.concatenate(given, axis=0))
 
@@ -641,10 +648,10 @@
                     hhid[...], wh[2 * pad :, cols], preferred_element_type=jnp.float32
                 )
                 for j in range(2):
-                    even = r[2 * j * half : (2 * j + 1) * half]
-                    odd = r[(2 * j + 1) * half : (2 * j + 2) * half]
-                    keep[here, j, lines, cols] = jnp.where(c == 0, even, odd)
-                    sc[here, j, lines, cols] = jnp.where(c == 0, odd, even).astype(jnp.bfloat16)
+                    keep[here, j, lines, cols] = r[j * half : (j + 1) * half]
+                    sc[here, j, lines, cols] = r[(2 + j) * half : (3 + j) * half].astype(
+                        jnp.bfloat16
+                    )
             share(here, h, 1 - y, t).start()
             share(here, h, y, t).start()
             hook(u, 4 + t)

time: 85.6 us -> 85.8 us (level)
  no operation moved by 1% of the time
where the time goes in v5:
time: 85.8 us; the launch traced here: 85.6 us
  Pallas kernels  83.7 us (98%)
  local copies, waits for them, and re-layouts  1.88 us (2%)
    pallas_call x1, Pallas kernels, shards(): pl.pallas_call(functools.partial(fused, n, hot, part), out_shape=jax.Shap...  83.7 us
    unnamed x1, local copies, waits for them, and re-layouts  1.88 us

profile of v5, /device:TPU:0, one launch (start us, length us, event | category | flops | bytes accessed | tf_op | source)
XLA Modules:
  0.0 85.6 jit_solution(15605666088020750472)
XLA Ops:
  0.0 83.7 %shard_map.100 = bf16[128,2048]{1,0:T(8,128)(2,1)} custom-call(bf16[128,2048]{1,0:T(8,128)(2,1)} %bitcast.14, s32[7,2,64]{2,1,0:T(2,128)} %bitcast.19, s32[2,64]{1,0:T(2,128)} %pick.1, f32[2,8,64]{2,1,0:T(8,128)} %bitcast.18, bf16[2048,768]{1,0:T(8,128)(2,1)} %bitcast.10, bf16[2048,768]{1,0:T(8,128)(2,1)} %bitcast.11, bf16[768,2048]{1,0:T(8,128)(2,1)} %bitcast.12, ...), custom_call_target="tpu_custom_call" | custom-call | tf_op jit(solution)/shard_map/pallas_call | solution.py:736
  83.7 1.9 %copy.12 = bf16[2,64,2048]{2,1,0:T(8,128)(2,1)} copy(bf16[2,64,2048]{2,1,0:T(8,128)(2,1)} %bitcast.13) | data formatting | bytes 1048576
